TPU v7x, 256 devices: a whole 4x4x8 slice. The times are simulated.
256 devices in a mesh: row: 16 (over x, y_hi, core), col: 8 (over z), depth: 2 (over y_lo).
Axes of the slice: x: 4, y: 4 (y_hi: 2, y_lo: 2; y = y_hi * 2 + y_lo), z: 8, core: 2. Of those that a mesh axis runs over, the one named last changes fastest.
Arguments:
- front_matrix: float32 [2, 8192, 8192], P('depth', 'row', 'col'), as said below
- block_mask: int32 [2, 64, 64], P('depth', 'row', 'col'), may hold values 0 or 1
- supernode_width: int32 [2, 3], P('depth'), may hold values from 128 to 256, as said below
Outputs:
- schur: float32 [2, 8192, 8192], P('depth', 'row', 'col')
- ancestor: float32 [4096, 4096], P('row', ('col', 'depth'))
Inputs may be any that keep to these rules, and one draw needn't show every extreme that they name: `front_matrix`: restricted to its first 768 rows and columns, each front is row diagonally dominant: each diagonal entry is positive and at least 1.5 times the sum of the magnitudes of the other entries of its row among those columns. `supernode_width`: each entry is a multiple of 128; in each front one supernode has the full width 256.
All inputs are finite; a program needn't handle non-finite values. No bound on the sum of `block_mask` on one device may be relied on, other than what follows from the above.
Results may differ from a plain program's by a relative error of at most 0.0001.
Values sent between devices are 32-bit elements; how exact they have to be, the bound alone decides.
No kernel may reach another device: no remote copies, remote signals or barrier semaphores. Data moves between devices by JAX's collectives and lax.ppermute only.
A program may use at most 64 MiB of HBM per device.

v0:
```python
import jax
import jax.numpy as jnp
from jax import lax
from jax.experimental import pallas as pl
from jax.experimental.pallas import tpu as pltpu
from jax.sharding import PartitionSpec as P


SN = 256
BLK = 128
NSN = 3
PIV = SN * NSN
ROWS = 16
COLS = 8
CHIPS = 8
XS = 4


def split(a):
    high = a.astype(jnp.bfloat16)
    low = (a - high.astype(jnp.float32)).astype(jnp.bfloat16)
    return high, low


def mul(a, b):
    return jnp.dot(a, b, preferred_element_type=jnp.float32)


def dot3(a, b):
    ah, al = a if isinstance(a, tuple) else split(a)
    bh, bl = b if isinstance(b, tuple) else split(b)
    return mul(ah, bh) + (mul(ah, bl) + mul(al, bh))


def inverse(block):
    shape = block.shape
    eye = lax.broadcasted_iota(jnp.int32, shape, 0) == lax.broadcasted_iota(jnp.int32, shape, 1)
    diagonal = jnp.where(eye, block, 0.0)
    by_row = 1.0 / jnp.sum(diagonal, axis=1, keepdims=True)
    by_col = 1.0 / jnp.sum(diagonal, axis=0, keepdims=True)
    power = jnp.where(eye, 0.0, -block * by_row)
    total = jnp.where(eye, 1.0, power)
    for _ in range(5):
        parts = split(power)
        power = dot3(parts, parts)
        total = total + dot3(total, power)
    return total * by_col


def place_rows(target, own, other, info):
    x, core = info[0], info[1]
    for parts, c in ((own, core), (other, 1 - core)):
        for k in range(XS):
            for e in range(2):
                chip = 2 * lax.rem(x + k, XS) + e
                target[pl.ds(pl.multiple_of(512 * c + 32 * chip, 32), 32), :] = parts[k][48 * e:48 * e + 32, :]
                target[pl.ds(pl.multiple_of(256 + 128 * c + 16 * chip, 16), 16), :] = parts[k][48 * e + 32:48 * e + 48, :]


def pieces_kernel(info, matrix, moved, *out):
    first = info[1] == 0
    for q in range(CHIPS):
        out[q][:32, :] = matrix[32 * q:32 * q + 32, :]
        mine = matrix[256 + 16 * q:272 + 16 * q, :]
        out[q][32:, :] = jnp.where(first, mine, moved[16 * q:16 * q + 16, :])


def factor_kernel(info, *refs):
    out, matrix = refs[8:]
    place_rows(matrix, refs[:4], refs[4:8], info)
    row_ids = lax.broadcasted_iota(jnp.int32, (SN, SN), 0)
    col_ids = lax.broadcasted_iota(jnp.int32, (SN, SN), 1)

    def block(i, j):
        keep = (row_ids < info[4 + i]) & (col_ids < info[4 + j])
        return jnp.where(keep, matrix[SN * i:SN * i + SN, SN * j:SN * j + SN], 0.0)

    def pivot(value, i):
        return jnp.where((row_ids == col_ids) & (row_ids >= info[4 + i]), 1.0, value)

    i0 = inverse(pivot(block(0, 0), 0))
    i0s = split(i0)
    v01 = split(dot3(i0s, block(0, 1)))
    v02 = split(dot3(i0s, block(0, 2)))
    m10 = split(block(1, 0))
    m20 = split(block(2, 0))
    i1 = inverse(pivot(block(1, 1) - dot3(m10, v01), 1))
    m12 = block(1, 2) - dot3(m10, v02)
    m21 = split(block(2, 1) - dot3(m20, v01))
    v12 = split(dot3(i1, m12))
    i2 = inverse(pivot(block(2, 2) - dot3(m20, v02) - dot3(m21, v12), 2))
    for n, value in enumerate((i0s, split(i1), split(i2), m10, m20, m21, v01, v02, v12)):
        out[2 * n] = value[0]
        out[2 * n + 1] = value[1]


def order_of(info, offset, axis, shape):
    ids = offset + lax.broadcasted_iota(jnp.int32, shape, axis)
    order = jnp.full(shape, NSN, jnp.int32)
    for s in range(NSN):
        order = jnp.where((ids >= SN * s) & (ids < SN * s + info[4 + s]), s, order)
    return order


def left_of(info, strips, got, left, panel):
    z = info[2]
    for k in range(COLS):
        place = lax.rem(z + k, COLS) * 64
        if k == 4:
            panel[pl.ds(pl.multiple_of(place, 64), 32), :] = strips[4][...]
            panel[pl.ds(pl.multiple_of(place + 32, 32), 32), :] = strips[5][...]
        else:
            panel[pl.ds(pl.multiple_of(place, 64), 64), :] = strips[k if k < 4 else k + 1][...]
    keep = lax.broadcasted_iota(jnp.int32, (512, SN), 1)
    order = order_of(info, info[3] * 512, 0, (512, 1))
    c = [jnp.where(keep < info[4 + s], panel[:, SN * s:SN * s + SN], 0.0) for s in range(NSN)]
    l0 = split(c[0])
    l1 = split(c[1] - dot3(l0, got(6)))
    l2 = split(c[2] - dot3(l0, got(7)) - dot3(l1, got(8)))
    for s, value in enumerate((l0, l1, l2)):
        live = order > s
        for part in range(2):
            left[part, :, SN * s:SN * s + SN] = jnp.where(live, value[part], jnp.zeros_like(value[part]))


def update_kernel(info, front, *refs, second):
    own, other, blocks = refs[:4], refs[4:8], refs[8]
    step = pl.program_id(0)

    def got(n):
        return blocks[2 * n], blocks[2 * n + 1]

    if second:
        left, _, out, quarter, band = refs[9:]
    else:
        strips, (out, quarter, left, band, panel) = refs[9:18], refs[18:]

        @pl.when(step == 0)
        def _():
            left_of(info, strips, got, left, panel)

    place_rows(band, own, other, info)
    width = band.shape[1]
    keep = lax.broadcasted_iota(jnp.int32, (SN, width), 0)
    r = [jnp.where(keep < info[4 + s], band[SN * s:SN * s + SN, :], 0.0) for s in range(NSN)]
    s0 = split(dot3(got(0), r[0]))
    s1 = split(dot3(got(1), r[1] - dot3(got(3), s0)))
    s2 = split(dot3(got(2), r[2] - dot3(got(4), s0) - dot3(got(5), s1)))
    half = info[8] if second else info[7]
    order = order_of(info, info[2] * 1024 + half * 512 + step * width, 1, (1, width))
    total = None
    for s, value in enumerate((s0, s1, s2)):
        live = order > s
        bh, bl = (jnp.where(live, part, jnp.zeros_like(part)) for part in value)
        ah = left[0, :, SN * s:SN * s + SN]
        al = left[1, :, SN * s:SN * s + SN]
        term = mul(ah, bh) + (mul(ah, bl) + mul(al, bh))
        total = term if total is None else total + term
    result = front[...] - total
    out[...] = result
    for i in range(2):
        for j in range(width // 256):
            quarter[128 * i:128 * i + 128, 128 * j:128 * j + 128] = result[
                256 * i + 128:256 * i + 256, 256 * j + 128:256 * j + 256
            ]


def each(axis_size, target):
    return [(i, target(i)) for i in range(axis_size)]


X_UP = each(ROWS, lambda i: (i + 4) % ROWS)
X_DOWN = each(ROWS, lambda i: (i - 4) % ROWS)
MATE = each(ROWS, lambda i: i ^ 2)
CORE = each(ROWS, lambda i: i ^ 1)
Z_UP = each(COLS, lambda i: (i + 1) % COLS)
Z_DOWN = each(COLS, lambda i: (i - 1) % COLS)
Z_ODD = [(z, z + 1) for z in range(0, COLS, 2)]


def gather_plane(piece, odd):
    height = piece.shape[0]
    mate = lax.ppermute(piece, "row", MATE)
    pair = jnp.concatenate([jnp.where(odd, mate, piece), jnp.where(odd, piece, mate)])
    before = lax.ppermute(pair, "row", X_UP)
    after = lax.ppermute(pair, "row", X_DOWN)
    far_even = lax.ppermute(before[:height], "row", X_UP)
    far_odd = lax.ppermute(after[height:], "row", X_DOWN)
    own = [pair, after, jnp.concatenate([far_even, far_odd]), before]
    return own, [lax.ppermute(part, "row", CORE) for part in own]


def gather_line(piece):
    half = piece.shape[0] // 2
    before, after = [piece], [piece]
    for _ in range(1, 4):
        before.append(lax.ppermute(before[-1], "col", Z_UP))
        after.append(lax.ppermute(after[-1], "col", Z_DOWN))
    far_high = lax.ppermute(before[3][:half], "col", Z_UP)
    far_low = lax.ppermute(after[3][half:], "col", Z_DOWN)
    return after[:4] + [far_high, far_low] + before[3:0:-1]


def exchange(matrix, info, row_index, col_index):
    odd = (row_index // 2) % 2 == 1
    odd_col = col_index % 2 == 1
    moved = lax.ppermute(matrix[384:512], "row", [(0, 1)])
    panel = matrix[:, :PIV]
    parts = [lax.ppermute(panel[64 * z:64 * z + 128], "col", [(0, z)]) for z in (2, 4, 6)]
    strip = jnp.where(col_index == 0, panel[:128], parts[0] + parts[1] + parts[2])
    strip = jnp.where(odd_col, lax.ppermute(strip[64:], "col", Z_ODD), strip[:64])

    pieces = pl.pallas_call(
        pieces_kernel,
        grid_spec=pltpu.PrefetchScalarGridSpec(
            num_scalar_prefetch=1,
            grid=(1,),
            in_specs=[pl.BlockSpec((384, 1024), lambda i, info: (0, 0)), pl.BlockSpec((128, 1024), lambda i, info: (0, 0))],
            out_specs=[pl.BlockSpec((48, 1024), lambda i, info: (0, 0))] * CHIPS,
        ),
        out_shape=[jax.ShapeDtypeStruct((48, 1024), jnp.float32)] * CHIPS,
        name="pieces",
    )(info, matrix, moved)
    parts = [lax.ppermute(pieces[q], "row", [(0, 2 * q), (1, 2 * q + 1)]) for q in range(1, CHIPS)]
    piece = jnp.where(row_index < 2, pieces[0], sum(parts[1:], parts[0]))

    core_piece = piece[:, :PIV]
    parts = [lax.ppermute(core_piece, "col", [(0, z)]) for z in (4, 2, 6)]
    pivot_piece = jnp.where(col_index == 0, core_piece, parts[0] + parts[1] + parts[2])
    pivot_piece = jnp.where(odd_col, lax.ppermute(pivot_piece, "col", Z_ODD), pivot_piece)

    return gather_plane(piece, odd), gather_plane(pivot_piece, odd), gather_line(strip)


def compute(info, matrix, band, pivot, strips):
    vmem = pl.BlockSpec(memory_space=pltpu.VMEM)
    blocks = pl.pallas_call(
        factor_kernel,
        grid_spec=pltpu.PrefetchScalarGridSpec(
            num_scalar_prefetch=1,
            grid=(),
            in_specs=[vmem] * 8,
            out_specs=vmem,
            scratch_shapes=[pltpu.VMEM((PIV, PIV), jnp.float32)],
        ),
        out_shape=jax.ShapeDtypeStruct((18, SN, SN), jnp.bfloat16),
        name="factor",
    )(info, *pivot[0], *pivot[1])

    width = 256

    def update(which, *inputs):
        def at(j, info):
            return (0, info[7 + which] * 2 + j)

        whole = lambda shape: pl.BlockSpec(shape, lambda j, info: (0,) * len(shape))
        left_shape = (2, 512, PIV)
        if which:
            specs = [whole(left_shape), pl.BlockSpec(memory_space=pl.ANY)]
        else:
            specs = [whole(value.shape) for value in inputs]
        return pl.pallas_call(
            lambda *refs: update_kernel(*refs, second=which == 1),
            grid_spec=pltpu.PrefetchScalarGridSpec(
                num_scalar_prefetch=1,
                grid=(2,),
                in_specs=[pl.BlockSpec((512, width), at)] + [pl.BlockSpec((96, width), at)] * 8 + [whole((18, SN, SN))] + specs,
                out_specs=[
                    pl.BlockSpec((512, width), at),
                    pl.BlockSpec((256, width // 2), lambda j, info: (0, j)),
                ] + [whole(left_shape)] * (1 - which),
                scratch_shapes=[pltpu.VMEM((PIV, width), jnp.float32)] + [pltpu.VMEM((512, PIV), jnp.float32)] * (1 - which),
            ),
            out_shape=[
                jax.ShapeDtypeStruct((512, 1024), jnp.float32),
                jax.ShapeDtypeStruct((256, 256), jnp.float32),
            ] + [jax.ShapeDtypeStruct(left_shape, jnp.bfloat16)] * (1 - which),
            input_output_aliases={12: 0} if which else {},
            name="update",
        )(info, matrix, *band[0], *band[1], blocks, *inputs)

    partial, leaving, left = update(0, *strips)
    arriving = lax.ppermute(leaving, "depth", [(0, 1), (1, 0)])
    result, staying = update(1, left, partial)
    return result[None], staying + arriving


def local(front_matrix, block_mask, supernode_width):
    row_index = lax.axis_index("row")
    col_index = lax.axis_index("col")
    depth_index = lax.axis_index("depth")
    block_rows = row_index * 4 + jnp.arange(4)
    block_cols = col_index * 8 + jnp.arange(8)
    kept = ((block_mask[0] != 0) | (block_rows[:, None] == block_cols[None, :])).astype(jnp.float32)
    kept = jnp.broadcast_to(kept[:, :, None], (4, 8, BLK)).reshape(4, 1, 1024)
    matrix = (front_matrix[0].reshape(4, BLK, 1024) * kept).reshape(512, 1024)
    info = jnp.concatenate([
        jnp.stack([row_index // 4, row_index % 2, col_index, row_index]).astype(jnp.int32),
        supernode_width[0],
        jnp.stack([1 - depth_index, depth_index]).astype(jnp.int32),
    ])
    panels = exchange(matrix, info, row_index, col_index)
    return compute(info, matrix, *panels)


def solution(mesh):
    placed = (P("depth", "row", "col"), P("depth", "row", "col"), P("depth", None))
    return jax.shard_map(
        local,
        mesh=mesh,
        in_specs=placed,
        out_specs=(P("depth", "row", "col"), P("row", ("col", "depth"))),
        check_vma=False,
    )
```

profile of v0, /device:TPU:1, one launch (start us, length us, event | category | flops | bytes accessed | tf_op | source)
XLA Modules:
  0.0 147.5 jit_solution(12291281120293066307)
XLA Ops:
  3.9 3.3 %bitcast_multiply_fusion.matrix.refs_1_ = f32[512,1024]{1,0:T(8,128)} fusion(f32[1,512,1024]{2,1,0:T(8,128)} %param.3, f32[4,1024]{1,0:T(4,128)S(1)} %bitcast.27), kind=kLoop, calls=%fused_computation | loop fusion | flops 524288 | bytes 4210688 | tf_op jit(solution)/shard_map/mul | solution.py:296
  9.3 3.3 %pieces.1 = (f32[48,1024]{1,0:T(8,128)}, f32[48,1024]{1,0:T(8,128)}, f32[48,1024]{1,0:T(8,128)}, f32[48,1024]{1,0:T(8,128)}, f32[48,1024]{1,0:T(8,128)}, /*index...) custom-call(s32[9]{0:T(128)} %concatenate.15.info.refs_0_, f32[512,1024]{1,0:T(8,128)} %bitcast_multiply_fusion.matrix.refs_1_, ...), custom_call_target="tpu_custom_call" | custom-call | tf_op jit(solution)/shard_map/pieces/pallas_call | solution.py:213
  12.6 4.6 %collective-permute-start.1 = (f32[48,1024]{1,0:T(8,128)}, f32[48,1024]{1,0:T(8,128)S(1)}, u32[]{:S(2)}, u32[]{:S(2)}) collective-permute-start(f32[48,1024]{1,0:T(8,128)} %get-tuple-element.16), channel_id=1, source_target_pairs={{0,32},{16,48},{1,33},{17,49},{2,34},{18,50},{3,35},{19,51},{4,36}... | collective-permute-start | bytes 589832 | tf_op jit(solution)/shard_map/ppermute | solution.py:224
  22.4 2.0 %collective-permute-start.6 = (f32[48,1024]{1,0:T(8,128)}, f32[48,1024]{1,0:T(8,128)}, u32[]{:S(2)}, u32[]{:S(2)}) collective-permute-start(f32[48,1024]{1,0:T(8,128)} %get-tuple-element.21), channel_id=1, source_target_pairs={{0,192},{16,208},{1,193},{17,209},{2,194},{18,210},{3,195},{19,211... | collective-permute-start | bytes 589832 | tf_op jit(solution)/shard_map/ppermute | solution.py:224
  25.1 2.0 %collective-permute-start.7 = (f32[48,1024]{1,0:T(8,128)}, f32[48,1024]{1,0:T(8,128)}, u32[]{:S(2)}, u32[]{:S(2)}) collective-permute-start(f32[48,1024]{1,0:T(8,128)} %get-tuple-element.22), channel_id=1, source_target_pairs={{0,224},{16,240},{1,225},{17,241},{2,226},{18,242},{3,227},{19,243... | collective-permute-start | bytes 589832 | tf_op jit(solution)/shard_map/ppermute | solution.py:224
  27.2 9.6 %collective-permute-start.31 = (f32[128,768]{1,0:T(8,128)S(1)}, f32[128,768]{1,0:T(8,128)}, u32[]{:S(2)}, u32[]{:S(2)}) collective-permute-start(f32[128,768]{1,0:T(8,128)S(1)} %get-tuple-element.28), channel_id=1, source_target_pairs={{0,8},{1,9},{16,24},{17,25},{32,40},{33,41},{48,56},{49,57},{64,72... | collective-permute-start | bytes 1179656 | tf_op jit(solution)/shard_map/ppermute | solution.py:209
  36.8 2.7 %collective-permute-start.32 = (f32[128,768]{1,0:T(8,128)S(1)}, f32[128,768]{1,0:T(8,128)}, u32[]{:S(2)}, u32[]{:S(2)}) collective-permute-start(f32[128,768]{1,0:T(8,128)S(1)} %get-tuple-element.29), channel_id=1, source_target_pairs={{0,12},{1,13},{16,28},{17,29},{32,44},{33,45},{48,60},{49,61},{64,... | collective-permute-start | bytes 1179656 | tf_op jit(solution)/shard_map/ppermute | solution.py:209
  40.2 2.0 %collective-permute-start.30 = (f32[128,768]{1,0:T(8,128)S(1)}, f32[128,768]{1,0:T(8,128)}, u32[]{:S(2)}, u32[]{:S(2)}) collective-permute-start(f32[128,768]{1,0:T(8,128)S(1)} %get-tuple-element.30), channel_id=1, source_target_pairs={{0,4},{1,5},{16,20},{17,21},{32,36},{33,37},{48,52},{49,53},{64,68... | collective-permute-start | bytes 1179656 | tf_op jit(solution)/shard_map/ppermute | solution.py:209
  42.2 1.5 %add_select_fusion = f32[48,1024]{1,0:T(8,128)S(1)} fusion(f32[48,1024]{1,0:T(8,128)S(1)} %copy-done.20, f32[48,1024]{1,0:T(8,128)} %collective-permute-done.7, f32[48,1024]{1,0:T(8,128)} %collective-permute-done.6, f32[48,1024]{1,0:T(8,128)} %copy-done.25, f32[48,1024]{1,0:T(8,128)} %copy-done.24, f32[48,1024]{1,0:T(8,128)} %copy-done.23, ...), kind=kLoop, calls=%fused_computation.7 | loop fusion | flops 344064 | bytes 1769473 | tf_op jit(solution)/shard_map/jit(_where)/select_n | solution.py:225
  43.7 2.8 %collective-permute-start.19 = (f32[48,768]{1,0:T(8,128)S(1)}, f32[48,768]{1,0:T(8,128)S(1)}, u32[]{:S(2)}, u32[]{:S(2)}) collective-permute-start(f32[48,768]{1,0:T(8,128)S(1)} %slice.69), channel_id=1, source_target_pairs={{0,12},{1,13},{16,28},{17,29},{32,44},{33,45},{48,60},{49,61},{64,... | collective-permute-start | bytes 442376 | tf_op jit(solution)/shard_map/ppermute | solution.py:228
  47.9 2.6 %collective-permute-start.17 = (f32[48,768]{1,0:T(8,128)S(1)}, f32[48,768]{1,0:T(8,128)S(1)}, u32[]{:S(2)}, u32[]{:S(2)}) collective-permute-start(f32[48,768]{1,0:T(8,128)S(1)} %slice.69), channel_id=1, source_target_pairs={{0,8},{1,9},{16,24},{17,25},{32,40},{33,41},{48,56},{49,57},{64,72... | collective-permute-start | bytes 442376 | tf_op jit(solution)/shard_map/ppermute | solution.py:228
  54.0 3.2 %collective-permute-done.17 = f32[48,768]{1,0:T(8,128)S(1)} collective-permute-done((f32[48,768]{1,0:T(8,128)S(1)}, f32[48,768]{1,0:T(8,128)S(1)}, u32[]{:S(2)}, u32[]{:S(2)}) %collective-permute-start.17) | collective-permute-done | bytes 147488 | tf_op jit(solution)/shard_map/ppermute | solution.py:228
  58.5 2.9 %collective-permute-done.33 = f32[64,768]{1,0:T(8,128)S(1)} collective-permute-done((f32[64,768]{1,0:T(8,128)S(1)}, f32[64,768]{1,0:T(8,128)S(1)}, u32[]{:S(2)}, u32[]{:S(2)}) %collective-permute-start.33) | collective-permute-done | bytes 196640 | tf_op jit(solution)/shard_map/ppermute | solution.py:211
  61.4 2.0 %collective-permute-start.37 = (f32[64,768]{1,0:T(8,128)S(1)}, f32[64,768]{1,0:T(8,128)S(1)}, u32[]{:S(2)}, u32[]{:S(2)}) collective-permute-start(f32[64,768]{1,0:T(8,128)S(1)} %slice_select_fusion.1.refs_11_), channel_id=1, source_target_pairs={{0,2},{2,4},{4,6},{6,8},{8,10},{10,12},{12,14},{14,0},{1,3},{3,5},... | collective-permute-start | bytes 589832 | tf_op jit(solution)/shard_map/ppermute | solution.py:197
  63.4 1.8 %collective-permute-start.8 = (f32[48,1024]{1,0:T(8,128)S(1)}, f32[48,1024]{1,0:T(8,128)S(1)}, u32[]{:S(2)}, u32[]{:S(2)}) collective-permute-start(f32[48,1024]{1,0:T(8,128)S(1)} %add_select_fusion), channel_id=1, source_target_pairs={{0,32},{16,48},{32,0},{48,16},{64,96},{80,112},{96,64},{112,80},{1... | collective-permute-start | bytes 589832 | tf_op jit(solution)/shard_map/ppermute | solution.py:183
  66.5 2.9 %collective-permute-done.8 = f32[48,1024]{1,0:T(8,128)S(1)} collective-permute-done((f32[48,1024]{1,0:T(8,128)S(1)}, f32[48,1024]{1,0:T(8,128)S(1)}, u32[]{:S(2)}, u32[]{:S(2)}) %collective-permute-start.8) | collective-permute-done | bytes 196640 | tf_op jit(solution)/shard_map/ppermute | solution.py:183
  71.6 2.1 %collective-permute-start.9 = (f32[96,1024]{1,0:T(8,128)S(1)}, f32[96,1024]{1,0:T(8,128)S(1)}, u32[]{:S(2)}, u32[]{:S(2)}) collective-permute-start(f32[96,1024]{1,0:T(8,128)S(1)} %pad_maximum_fusion.refs_2_), channel_id=1, source_target_pairs={{0,192},{16,208},{32,224},{48,240},{64,0},{80,16},{96,32},{112,48}... | collective-permute-start | bytes 1179656 | tf_op jit(solution)/shard_map/ppermute | solution.py:186
  73.9 3.1 %collective-permute-done.38.refs_18_ = f32[64,768]{1,0:T(8,128)S(1)} collective-permute-done((f32[64,768]{1,0:T(8,128)S(1)}, f32[64,768]{1,0:T(8,128)S(1)}, u32[]{:S(2)}, u32[]{:S(2)}) %collective-permute-start.38) | collective-permute-done | bytes 196640 | tf_op jit(solution)/shard_map/ppermute | solution.py:197
  77.0 1.8 %collective-permute-start.22 = (f32[96,768]{1,0:T(8,128)S(1)}, f32[96,768]{1,0:T(8,128)S(1)}, u32[]{:S(2)}, u32[]{:S(2)}) collective-permute-start(f32[96,768]{1,0:T(8,128)S(1)} %pad_maximum_fusion.1.refs_0_), channel_id=1, source_target_pairs={{0,192},{16,208},{32,224},{48,240},{64,0},{80,16},{96,32},{112,48}... | collective-permute-start | bytes 884744 | tf_op jit(solution)/shard_map/ppermute | solution.py:186
  78.9 2.7 %collective-permute-start.35 = (f32[64,768]{1,0:T(8,128)S(1)}, f32[64,768]{1,0:T(8,128)S(1)}, u32[]{:S(2)}, u32[]{:S(2)}) collective-permute-start(f32[64,768]{1,0:T(8,128)S(1)} %collective-permute-done.34.refs_12_), channel_id=1, source_target_pairs={{0,14},{2,0},{4,2},{6,4},{8,6},{10,8},{12,10},{14,12},{1,15},{3,1}... | collective-permute-start | bytes 589832 | tf_op jit(solution)/shard_map/ppermute | solution.py:198
  81.7 4.2 %collective-permute-done.39.refs_17_ = f32[64,768]{1,0:T(8,128)S(1)} collective-permute-done((f32[64,768]{1,0:T(8,128)S(1)}, f32[64,768]{1,0:T(8,128)S(1)}, u32[]{:S(2)}, u32[]{:S(2)}) %collective-permute-start.39) | collective-permute-done | bytes 196640 | tf_op jit(solution)/shard_map/ppermute | solution.py:197
  86.0 9.5 %collective-permute-start.26 = (f32[96,768]{1,0:T(8,128)S(1)}, f32[96,768]{1,0:T(8,128)}, u32[]{:S(2)}, u32[]{:S(2)}) collective-permute-start(f32[96,768]{1,0:T(8,128)S(1)} %pad_maximum_fusion.1.refs_0_), channel_id=1, source_target_pairs={{0,16},{16,0},{32,48},{48,32},{64,80},{80,64},{96,112},{112,96},{1... | collective-permute-start | bytes 884744 | tf_op jit(solution)/shard_map/ppermute | solution.py:190
  95.5 1.3 collective-permute-start.24
  96.9 1.5 %collective-permute-start.25 = (f32[48,768]{1,0:T(8,128)S(1)}, f32[48,768]{1,0:T(8,128)S(1)}, u32[]{:S(2)}, u32[]{:S(2)}) collective-permute-start(f32[48,768]{1,0:T(8,128)S(1)} %slice.71), channel_id=1, source_target_pairs={{0,192},{16,208},{32,224},{48,240},{64,0},{80,16},{96,32},{112,48}... | collective-permute-start | bytes 442376 | tf_op jit(solution)/shard_map/ppermute | solution.py:188
  99.1 1.6 %collective-permute-start.27 = (f32[96,768]{1,0:T(8,128)S(1)}, f32[96,768]{1,0:T(8,128)S(1)}, u32[]{:S(2)}, u32[]{:S(2)}) collective-permute-start(f32[96,768]{1,0:T(8,128)S(1)} %collective-permute-done.22.refs_1_), channel_id=1, source_target_pairs={{0,16},{16,0},{32,48},{48,32},{64,80},{80,64},{96,112},{112,96},{1... | collective-permute-start | bytes 884744 | tf_op jit(solution)/shard_map/ppermute | solution.py:190
  100.7 1.5 %collective-permute-done.24 = f32[48,768]{1,0:T(8,128)S(1)} collective-permute-done((f32[48,768]{1,0:T(8,128)S(1)}, f32[48,768]{1,0:T(8,128)S(1)}, u32[]{:S(2)}, u32[]{:S(2)}) %collective-permute-start.24) | collective-permute-done | bytes 147488 | tf_op jit(solution)/shard_map/ppermute | solution.py:187
  103.8 4.0 %collective-permute-done.36.refs_14_ = f32[64,768]{1,0:T(8,128)S(1)} collective-permute-done((f32[64,768]{1,0:T(8,128)S(1)}, f32[64,768]{1,0:T(8,128)S(1)}, u32[]{:S(2)}, u32[]{:S(2)}) %collective-permute-start.36) | collective-permute-done | bytes 196640 | tf_op jit(solution)/shard_map/ppermute | solution.py:198
  107.8 1.7 %collective-permute-start.13 = (f32[96,1024]{1,0:T(8,128)S(1)}, f32[96,1024]{1,0:T(8,128)S(1)}, u32[]{:S(2)}, u32[]{:S(2)}) collective-permute-start(f32[96,1024]{1,0:T(8,128)S(1)} %pad_maximum_fusion.refs_2_), channel_id=1, source_target_pairs={{0,16},{16,0},{32,48},{48,32},{64,80},{80,64},{96,112},{112,96},{1... | collective-permute-start | bytes 1179656 | tf_op jit(solution)/shard_map/ppermute | solution.py:190
  113.4 11.4 %factor.1.refs_10_ = bf16[18,256,256]{2,1,0:T(8,128)(2,1)} custom-call(s32[9]{0:T(128)} %concatenate.15.info.refs_0_, f32[96,768]{1,0:T(8,128)} %copy-done.9, f32[96,768]{1,0:T(8,128)} %copy-done.12, f32[96,768]{1,0:T(8,128)} %copy-done.13, f32[96,768]{1,0:T(8,128)} %copy-done.11, f32[96,768]{1,0:T(8,128)} %collective-permute-done.26.refs_4_, ...), custom_call_target="tpu_custom_call" | custom-call | tf_op jit(solution)/shard_map/factor/pallas_call | solution.py:237
  126.7 9.8 %update.2 = (f32[512,1024]{1,0:T(8,128)}, f32[256,256]{1,0:T(8,128)}, bf16[2,512,768]{2,1,0:T(8,128)(2,1)}) custom-call(s32[9]{0:T(128)} %concatenate.15.info.refs_0_, f32[512,1024]{1,0:T(8,128)} %bitcast_multiply_fusion.matrix.refs_1_, f32[96,1024]{1,0:T(8,128)} %copy-done.1, f32[96,1024]{1,0:T(8,128)} %copy-done.3, f32[96,1024]{1,0:T(8,128)} %copy-done.4, ...), custom_call_target="tpu_custom_call" | custom-call | tf_op jit(solution)/shard_map/update/pallas_call | solution.py:262
  137.0 8.9 %update.3 = (f32[512,1024]{1,0:T(8,128)}, f32[256,256]{1,0:T(8,128)}) custom-call(s32[9]{0:T(128)} %concatenate.15.info.refs_0_, f32[512,1024]{1,0:T(8,128)} %bitcast_multiply_fusion.matrix.refs_1_, f32[96,1024]{1,0:T(8,128)} %copy-done.1, f32[96,1024]{1,0:T(8,128)} %copy-done.3, f32[96,1024]{1,0:T(8,128)} %copy-done.4, ...), custom_call_target="tpu_custom_call", output_to_operand_aliasing={{0}: (12, {})} | custom-call | tf_op jit(solution)/shard_map/update/pallas_call | solution.py:262
  145.9 1.7 %add.82 = f32[256,256]{1,0:T(8,128)} add(f32[256,256]{1,0:T(8,128)} %get-tuple-element.26, f32[256,256]{1,0:T(8,128)S(1)} %collective-permute-done.42) | non-fusion elementwise | flops 65536 | bytes 786432 | tf_op jit(solution)/shard_map/add | solution.py:285
  (154 shorter events, 30.3 us)
Async XLA Ops:
  12.6 9.8 %collective-permute-start.1 = (f32[48,1024]{1,0:T(8,128)}, f32[48,1024]{1,0:T(8,128)S(1)}, u32[]{:S(2)}, u32[]{:S(2)}) collective-permute-start(f32[48,1024]{1,0:T(8,128)} %get-tuple-element.16), channel_id=1, source_target_pairs={{0,32},{16,48},{1,33},{17,49},{2,34},{18,50},{3,35},{19,51},{4,36}... | collective-permute-start | bytes 589832 | tf_op jit(solution)/shard_map/ppermute | solution.py:224
  18.5 8.7 %collective-permute-start.3 = (f32[48,1024]{1,0:T(8,128)}, f32[48,1024]{1,0:T(8,128)S(1)}, u32[]{:S(2)}, u32[]{:S(2)}) collective-permute-start(f32[48,1024]{1,0:T(8,128)} %get-tuple-element.18), channel_id=1, source_target_pairs={{0,96},{16,112},{1,97},{17,113},{2,98},{18,114},{3,99},{19,115},{4... | collective-permute-start | bytes 589832 | tf_op jit(solution)/shard_map/ppermute | solution.py:224
  19.8 17.0 %collective-permute-start.4 = (f32[48,1024]{1,0:T(8,128)}, f32[48,1024]{1,0:T(8,128)S(1)}, u32[]{:S(2)}, u32[]{:S(2)}) collective-permute-start(f32[48,1024]{1,0:T(8,128)} %get-tuple-element.19), channel_id=1, source_target_pairs={{0,128},{16,144},{1,129},{17,145},{2,130},{18,146},{3,131},{19,147... | collective-permute-start | bytes 589832 | tf_op jit(solution)/shard_map/ppermute | solution.py:224
  21.1 18.4 %collective-permute-start.5 = (f32[48,1024]{1,0:T(8,128)}, f32[48,1024]{1,0:T(8,128)S(1)}, u32[]{:S(2)}, u32[]{:S(2)}) collective-permute-start(f32[48,1024]{1,0:T(8,128)} %get-tuple-element.20), channel_id=1, source_target_pairs={{0,160},{16,176},{1,161},{17,177},{2,162},{18,178},{3,163},{19,179... | collective-permute-start | bytes 589832 | tf_op jit(solution)/shard_map/ppermute | solution.py:224
  22.4 19.8 %collective-permute-start.6 = (f32[48,1024]{1,0:T(8,128)}, f32[48,1024]{1,0:T(8,128)}, u32[]{:S(2)}, u32[]{:S(2)}) collective-permute-start(f32[48,1024]{1,0:T(8,128)} %get-tuple-element.21), channel_id=1, source_target_pairs={{0,192},{16,208},{1,193},{17,209},{2,194},{18,210},{3,195},{19,211... | collective-permute-start | bytes 589832 | tf_op jit(solution)/shard_map/ppermute | solution.py:224
  25.1 17.1 %collective-permute-start.7 = (f32[48,1024]{1,0:T(8,128)}, f32[48,1024]{1,0:T(8,128)}, u32[]{:S(2)}, u32[]{:S(2)}) collective-permute-start(f32[48,1024]{1,0:T(8,128)} %get-tuple-element.22), channel_id=1, source_target_pairs={{0,224},{16,240},{1,225},{17,241},{2,226},{18,242},{3,227},{19,243... | collective-permute-start | bytes 589832 | tf_op jit(solution)/shard_map/ppermute | solution.py:224
  27.2 20.7 %collective-permute-start.31 = (f32[128,768]{1,0:T(8,128)S(1)}, f32[128,768]{1,0:T(8,128)}, u32[]{:S(2)}, u32[]{:S(2)}) collective-permute-start(f32[128,768]{1,0:T(8,128)S(1)} %get-tuple-element.28), channel_id=1, source_target_pairs={{0,8},{1,9},{16,24},{17,25},{32,40},{33,41},{48,56},{49,57},{64,72... | collective-permute-start | bytes 1179656 | tf_op jit(solution)/shard_map/ppermute | solution.py:209
  36.8 13.8 %collective-permute-start.32 = (f32[128,768]{1,0:T(8,128)S(1)}, f32[128,768]{1,0:T(8,128)}, u32[]{:S(2)}, u32[]{:S(2)}) collective-permute-start(f32[128,768]{1,0:T(8,128)S(1)} %get-tuple-element.29), channel_id=1, source_target_pairs={{0,12},{1,13},{16,28},{17,29},{32,44},{33,45},{48,60},{49,61},{64,... | collective-permute-start | bytes 1179656 | tf_op jit(solution)/shard_map/ppermute | solution.py:209
  40.2 10.7 %collective-permute-start.30 = (f32[128,768]{1,0:T(8,128)S(1)}, f32[128,768]{1,0:T(8,128)}, u32[]{:S(2)}, u32[]{:S(2)}) collective-permute-start(f32[128,768]{1,0:T(8,128)S(1)} %get-tuple-element.30), channel_id=1, source_target_pairs={{0,4},{1,5},{16,20},{17,21},{32,36},{33,37},{48,52},{49,53},{64,68... | collective-permute-start | bytes 1179656 | tf_op jit(solution)/shard_map/ppermute | solution.py:209
  43.7 9.8 %collective-permute-start.19 = (f32[48,768]{1,0:T(8,128)S(1)}, f32[48,768]{1,0:T(8,128)S(1)}, u32[]{:S(2)}, u32[]{:S(2)}) collective-permute-start(f32[48,768]{1,0:T(8,128)S(1)} %slice.69), channel_id=1, source_target_pairs={{0,12},{1,13},{16,28},{17,29},{32,44},{33,45},{48,60},{49,61},{64,... | collective-permute-start | bytes 442376 | tf_op jit(solution)/shard_map/ppermute | solution.py:228
  46.6 7.4 %collective-permute-start.18 = (f32[48,768]{1,0:T(8,128)S(1)}, f32[48,768]{1,0:T(8,128)S(1)}, u32[]{:S(2)}, u32[]{:S(2)}) collective-permute-start(f32[48,768]{1,0:T(8,128)S(1)} %slice.69), channel_id=1, source_target_pairs={{0,4},{1,5},{16,20},{17,21},{32,36},{33,37},{48,52},{49,53},{64,68... | collective-permute-start | bytes 442376 | tf_op jit(solution)/shard_map/ppermute | solution.py:228
  47.9 9.3 %collective-permute-start.17 = (f32[48,768]{1,0:T(8,128)S(1)}, f32[48,768]{1,0:T(8,128)S(1)}, u32[]{:S(2)}, u32[]{:S(2)}) collective-permute-start(f32[48,768]{1,0:T(8,128)S(1)} %slice.69), channel_id=1, source_target_pairs={{0,8},{1,9},{16,24},{17,25},{32,40},{33,41},{48,56},{49,57},{64,72... | collective-permute-start | bytes 442376 | tf_op jit(solution)/shard_map/ppermute | solution.py:228
  52.2 9.2 %collective-permute-start.33 = (f32[64,768]{1,0:T(8,128)S(1)}, f32[64,768]{1,0:T(8,128)S(1)}, u32[]{:S(2)}, u32[]{:S(2)}) collective-permute-start(f32[64,768]{1,0:T(8,128)S(1)} %slice.76), channel_id=1, source_target_pairs={{0,2},{4,6},{8,10},{12,14},{1,3},{5,7},{9,11},{13,15},{16,18},{20,... | collective-permute-start | bytes 589832 | tf_op jit(solution)/shard_map/ppermute | solution.py:211
  57.2 8.0 %collective-permute-start.20 = (f32[48,768]{1,0:T(8,128)S(1)}, f32[48,768]{1,0:T(8,128)S(1)}, u32[]{:S(2)}, u32[]{:S(2)}) collective-permute-start(f32[48,768]{1,0:T(8,128)S(1)} %add_select_fusion.1), channel_id=1, source_target_pairs={{0,2},{4,6},{8,10},{12,14},{1,3},{5,7},{9,11},{13,15},{16,18},{20,... | collective-permute-start | bytes 442376 | tf_op jit(solution)/shard_map/ppermute | solution.py:230
  61.4 9.5 %collective-permute-start.37 = (f32[64,768]{1,0:T(8,128)S(1)}, f32[64,768]{1,0:T(8,128)S(1)}, u32[]{:S(2)}, u32[]{:S(2)}) collective-permute-start(f32[64,768]{1,0:T(8,128)S(1)} %slice_select_fusion.1.refs_11_), channel_id=1, source_target_pairs={{0,2},{2,4},{4,6},{6,8},{8,10},{10,12},{12,14},{14,0},{1,3},{3,5},... | collective-permute-start | bytes 589832 | tf_op jit(solution)/shard_map/ppermute | solution.py:197
  65.2 8.6 %collective-permute-start.21 = (f32[48,768]{1,0:T(8,128)S(1)}, f32[48,768]{1,0:T(8,128)S(1)}, u32[]{:S(2)}, u32[]{:S(2)}) collective-permute-start(f32[48,768]{1,0:T(8,128)S(1)} %broadcast_select_fusion.2), channel_id=1, source_target_pairs={{0,32},{16,48},{32,0},{48,16},{64,96},{80,112},{96,64},{112,80},{1... | collective-permute-start | bytes 442376 | tf_op jit(solution)/shard_map/ppermute | solution.py:183
  69.5 9.3 %collective-permute-start.10 = (f32[96,1024]{1,0:T(8,128)S(1)}, f32[96,1024]{1,0:T(8,128)S(1)}, u32[]{:S(2)}, u32[]{:S(2)}) collective-permute-start(f32[96,1024]{1,0:T(8,128)S(1)} %pad_maximum_fusion.refs_2_), channel_id=1, source_target_pairs={{0,64},{16,80},{32,96},{48,112},{64,128},{80,144},{96,160},{112,17... | collective-permute-start | bytes 1179656 | tf_op jit(solution)/shard_map/ppermute | solution.py:185
  70.2 8.6 %collective-permute-start.34 = (f32[64,768]{1,0:T(8,128)S(1)}, f32[64,768]{1,0:T(8,128)S(1)}, u32[]{:S(2)}, u32[]{:S(2)}) collective-permute-start(f32[64,768]{1,0:T(8,128)S(1)} %slice_select_fusion.1.refs_11_), channel_id=1, source_target_pairs={{0,14},{2,0},{4,2},{6,4},{8,6},{10,8},{12,10},{14,12},{1,15},{3,1}... | collective-permute-start | bytes 589832 | tf_op jit(solution)/shard_map/ppermute | solution.py:198
  73.8 12.2 %collective-permute-start.23 = (f32[96,768]{1,0:T(8,128)S(1)}, f32[96,768]{1,0:T(8,128)S(1)}, u32[]{:S(2)}, u32[]{:S(2)}) collective-permute-start(f32[96,768]{1,0:T(8,128)S(1)} %pad_maximum_fusion.1.refs_0_), channel_id=1, source_target_pairs={{0,64},{16,80},{32,96},{48,112},{64,128},{80,144},{96,160},{112,17... | collective-permute-start | bytes 884744 | tf_op jit(solution)/shard_map/ppermute | solution.py:185
  77.0 18.5 %collective-permute-start.22 = (f32[96,768]{1,0:T(8,128)S(1)}, f32[96,768]{1,0:T(8,128)S(1)}, u32[]{:S(2)}, u32[]{:S(2)}) collective-permute-start(f32[96,768]{1,0:T(8,128)S(1)} %pad_maximum_fusion.1.refs_0_), channel_id=1, source_target_pairs={{0,192},{16,208},{32,224},{48,240},{64,0},{80,16},{96,32},{112,48}... | collective-permute-start | bytes 884744 | tf_op jit(solution)/shard_map/ppermute | solution.py:186
  78.8 18.0 %collective-permute-start.11 = (f32[48,1024]{1,0:T(8,128)S(1)}, f32[48,1024]{1,0:T(8,128)S(1)}, u32[]{:S(2)}, u32[]{:S(2)}) collective-permute-start(f32[48,1024]{1,0:T(8,128)S(1)} %slice.67), channel_id=1, source_target_pairs={{0,64},{16,80},{32,96},{48,112},{64,128},{80,144},{96,160},{112,17... | collective-permute-start | bytes 589832 | tf_op jit(solution)/shard_map/ppermute | solution.py:187
  78.9 19.5 %collective-permute-start.35 = (f32[64,768]{1,0:T(8,128)S(1)}, f32[64,768]{1,0:T(8,128)S(1)}, u32[]{:S(2)}, u32[]{:S(2)}) collective-permute-start(f32[64,768]{1,0:T(8,128)S(1)} %collective-permute-done.34.refs_12_), channel_id=1, source_target_pairs={{0,14},{2,0},{4,2},{6,4},{8,6},{10,8},{12,10},{14,12},{1,15},{3,1}... | collective-permute-start | bytes 589832 | tf_op jit(solution)/shard_map/ppermute | solution.py:198
  85.9 13.1 %collective-permute-start.12 = (f32[48,1024]{1,0:T(8,128)S(1)}, f32[48,1024]{1,0:T(8,128)S(1)}, u32[]{:S(2)}, u32[]{:S(2)}) collective-permute-start(f32[48,1024]{1,0:T(8,128)S(1)} %slice.68), channel_id=1, source_target_pairs={{0,192},{16,208},{32,224},{48,240},{64,0},{80,16},{96,32},{112,48}... | collective-permute-start | bytes 589832 | tf_op jit(solution)/shard_map/ppermute | solution.py:188
  86.0 23.6 %collective-permute-start.26 = (f32[96,768]{1,0:T(8,128)S(1)}, f32[96,768]{1,0:T(8,128)}, u32[]{:S(2)}, u32[]{:S(2)}) collective-permute-start(f32[96,768]{1,0:T(8,128)S(1)} %pad_maximum_fusion.1.refs_0_), channel_id=1, source_target_pairs={{0,16},{16,0},{32,48},{48,32},{64,80},{80,64},{96,112},{112,96},{1... | collective-permute-start | bytes 884744 | tf_op jit(solution)/shard_map/ppermute | solution.py:190
  98.4 11.6 %collective-permute-start.29 = (f32[96,768]{1,0:T(8,128)S(1)}, f32[96,768]{1,0:T(8,128)S(1)}, u32[]{:S(2)}, u32[]{:S(2)}) collective-permute-start(f32[96,768]{1,0:T(8,128)S(1)} %collective-permute-done.23.refs_3_), channel_id=1, source_target_pairs={{0,16},{16,0},{32,48},{48,32},{64,80},{80,64},{96,112},{112,96},{1... | collective-permute-start | bytes 884744 | tf_op jit(solution)/shard_map/ppermute | solution.py:190
  99.1 11.1 %collective-permute-start.27 = (f32[96,768]{1,0:T(8,128)S(1)}, f32[96,768]{1,0:T(8,128)S(1)}, u32[]{:S(2)}, u32[]{:S(2)}) collective-permute-start(f32[96,768]{1,0:T(8,128)S(1)} %collective-permute-done.22.refs_1_), channel_id=1, source_target_pairs={{0,16},{16,0},{32,48},{48,32},{64,80},{80,64},{96,112},{112,96},{1... | collective-permute-start | bytes 884744 | tf_op jit(solution)/shard_map/ppermute | solution.py:190
  107.8 17.1 %collective-permute-start.13 = (f32[96,1024]{1,0:T(8,128)S(1)}, f32[96,1024]{1,0:T(8,128)S(1)}, u32[]{:S(2)}, u32[]{:S(2)}) collective-permute-start(f32[96,1024]{1,0:T(8,128)S(1)} %pad_maximum_fusion.refs_2_), channel_id=1, source_target_pairs={{0,16},{16,0},{32,48},{48,32},{64,80},{80,64},{96,112},{112,96},{1... | collective-permute-start | bytes 1179656 | tf_op jit(solution)/shard_map/ppermute | solution.py:190
  109.6 15.2 %collective-permute-start.16 = (f32[96,1024]{1,0:T(8,128)S(1)}, f32[96,1024]{1,0:T(8,128)S(1)}, u32[]{:S(2)}, u32[]{:S(2)}) collective-permute-start(f32[96,1024]{1,0:T(8,128)S(1)} %collective-permute-done.10.refs_5_), channel_id=1, source_target_pairs={{0,16},{16,0},{32,48},{48,32},{64,80},{80,64},{96,112},{112,96},{1... | collective-permute-start | bytes 1179656 | tf_op jit(solution)/shard_map/ppermute | solution.py:190
  110.0 14.8 %collective-permute-start.14 = (f32[96,1024]{1,0:T(8,128)S(1)}, f32[96,1024]{1,0:T(8,128)S(1)}, u32[]{:S(2)}, u32[]{:S(2)}) collective-permute-start(f32[96,1024]{1,0:T(8,128)S(1)} %collective-permute-done.9.refs_3_), channel_id=1, source_target_pairs={{0,16},{16,0},{32,48},{48,32},{64,80},{80,64},{96,112},{112,96},{1... | collective-permute-start | bytes 1179656 | tf_op jit(solution)/shard_map/ppermute | solution.py:190
  110.2 14.7 %collective-permute-start.15 = (f32[96,1024]{1,0:T(8,128)S(1)}, f32[96,1024]{1,0:T(8,128)S(1)}, u32[]{:S(2)}, u32[]{:S(2)}) collective-permute-start(f32[96,1024]{1,0:T(8,128)S(1)} %constant_dynamic-update-slice_fusion.refs_4_), channel_id=1, source_target_pairs={{0,16},{16,0},{32,48},{48,32},{64,80},{80,64},{96,112},{112,96},{1... | collective-permute-start | bytes 1179656 | tf_op jit(solution)/shard_map/ppermute | solution.py:190
  112.2 12.6 %collective-permute-start.41 = (f32[32,768]{1,0:T(8,128)}, f32[32,768]{1,0:T(8,128)}, u32[]{:S(2)}, u32[]{:S(2)}) collective-permute-start(f32[32,768]{1,0:T(8,128)} %slice.79), channel_id=1, source_target_pairs={{0,14},{2,0},{4,2},{6,4},{8,6},{10,8},{12,10},{14,12},{1,15},{3,1}... | collective-permute-start | bytes 294920 | tf_op jit(solution)/shard_map/ppermute | solution.py:200
  136.5 9.4 %collective-permute-start.42 = (f32[256,256]{1,0:T(8,128)}, f32[256,256]{1,0:T(8,128)S(1)}, u32[]{:S(2)}, u32[]{:S(2)}) collective-permute-start(f32[256,256]{1,0:T(8,128)} %get-tuple-element.27), channel_id=1, source_target_pairs={{0,1},{1,0},{2,3},{3,2},{4,5},{5,4},{6,7},{7,6},{8,9},{9,8},{10,11... | collective-permute-start | bytes 786440 | tf_op jit(solution)/shard_map/ppermute | solution.py:283
  (43 other events, 543.7 us)
where the time goes:
time: 148 us
  starting transfers between devices  72.9 us (49%)
  Pallas kernels  33.4 us (23%)
  waiting for transfers between devices  23.7 us (16%)
  other arithmetic  9.79 us (7%)
  local copies, waits for them, and re-layouts  6.36 us (4%)
    pallas_call x2, Pallas kernels, update(): pl.pallas_call(lambda *refs: update_kernel(*refs, second=which == 1), gri...  18.7 us
    ppermute x8, starting transfers between devices, gather_plane(): return (own, [lax.ppermute(part, 'row', CORE) for part in own])  14.6 us
    ppermute x3, starting transfers between devices, exchange(): lax.ppermute(panel[64 * z:64 * z + 128], 'col', [(0, z)])  14.3 us
    ppermute x7, starting transfers between devices, exchange(): lax.ppermute(pieces[q], 'row', [(0, 2 * q), (1, 2 * q + 1)])  13.7 us
    pallas_call x1, Pallas kernels, compute(): pl.pallas_call(factor_kernel, grid_spec=pltpu.PrefetchScalarGridSpec(num_...  11.4 us
    ppermute x3, waiting for transfers between devices, gather_line(): before.append(lax.ppermute(before[-1], 'col', Z_UP))  7.31 us
    ppermute x3, starting transfers between devices, exchange(): parts = [lax.ppermute(core_piece, 'col', [(0, z)]) for z in (4, 2, 6)]  6.78 us
    unnamed x68, local copies, waits for them, and re-layouts  4.85 us
  transfers between devices with their start and end apart: 43, of which 11 were waited for; matrix products, arithmetic and copies ran while one was open for 5% of the time, Pallas kernels for 14%

commit v1 on v0

--- a/solution.py
+++ b/solution.py
@@ -26,10 +26,14 @@
     return jnp.dot(a, b, preferred_element_type=jnp.float32)
 
 
+def stack(a):
+    return jnp.concatenate(split(a), axis=0)
+
+
 def dot3(a, b):
-    ah, al = a if isinstance(a, tuple) else split(a)
-    bh, bl = b if isinstance(b, tuple) else split(b)
-    return mul(ah, bh) + (mul(ah, bl) + mul(al, bh))
+    rows = a.shape[0] // 2
+    both = mul(a, b[0])
+    return both[:rows] + (both[rows:] + mul(a[:rows], b[1]))
 
 
 def inverse(block):
@@ -42,19 +46,19 @@
     total = jnp.where(eye, 1.0, power)
     for _ in range(5):
         parts = split(power)
-        power = dot3(parts, parts)
-        total = total + dot3(total, power)
+        power = dot3(jnp.concatenate(parts, axis=0), parts)
+        total = total + dot3(stack(total), split(power))
     return total * by_col
 
 
-def place_rows(target, own, other, info):
+def place_rows(target, own, other, info, columns=slice(None)):
     x, core = info[0], info[1]
     for parts, c in ((own, core), (other, 1 - core)):
         for k in range(XS):
             for e in range(2):
                 chip = 2 * lax.rem(x + k, XS) + e
-                target[pl.ds(pl.multiple_of(512 * c + 32 * chip, 32), 32), :] = parts[k][48 * e:48 * e + 32, :]
-                target[pl.ds(pl.multiple_of(256 + 128 * c + 16 * chip, 16), 16), :] = parts[k][48 * e + 32:48 * e + 48, :]
+                target[pl.ds(pl.multiple_of(512 * c + 32 * chip, 32), 32), :] = parts[k][48 * e:48 * e + 32, columns]
+                target[pl.ds(pl.multiple_of(256 + 128 * c + 16 * chip, 16), 16), :] = parts[k][48 * e + 32:48 * e + 48, columns]
 
 
 def pieces_kernel(info, matrix, moved, *out):
@@ -78,20 +82,21 @@
     def pivot(value, i):
         return jnp.where((row_ids == col_ids) & (row_ids >= info[4 + i]), 1.0, value)
 
-    i0 = inverse(pivot(block(0, 0), 0))
-    i0s = split(i0)
-    v01 = split(dot3(i0s, block(0, 1)))
-    v02 = split(dot3(i0s, block(0, 2)))
-    m10 = split(block(1, 0))
-    m20 = split(block(2, 0))
-    i1 = inverse(pivot(block(1, 1) - dot3(m10, v01), 1))
+    i0 = stack(inverse(pivot(block(0, 0), 0)))
+    v01 = split(dot3(i0, split(block(0, 1))))
+    v02 = split(dot3(i0, split(block(0, 2))))
+    m10 = stack(block(1, 0))
+    m20 = stack(block(2, 0))
+    i1 = stack(inverse(pivot(block(1, 1) - dot3(m10, v01), 1)))
     m12 = block(1, 2) - dot3(m10, v02)
-    m21 = split(block(2, 1) - dot3(m20, v01))
-    v12 = split(dot3(i1, m12))
-    i2 = inverse(pivot(block(2, 2) - dot3(m20, v02) - dot3(m21, v12), 2))
-    for n, value in enumerate((i0s, split(i1), split(i2), m10, m20, m21, v01, v02, v12)):
-        out[2 * n] = value[0]
-        out[2 * n + 1] = value[1]
+    m21 = stack(block(2, 1) - dot3(m20, v01))
+    v12 = split(dot3(i1, split(m12)))
+    i2 = stack(inverse(pivot(block(2, 2) - dot3(m20, v02) - dot3(m21, v12), 2)))
+    for n, value in enumerate((i0, i1, i2, m10, m20, m21)):
+        out[n] = value
+    for n, value in enumerate((v01, v02, v12)):
+        out[6 + n, :SN] = value[0]
+        out[6 + n, SN:] = value[1]
 
 
 def order_of(info, offset, axis, shape):
@@ -114,13 +119,12 @@
     keep = lax.broadcasted_iota(jnp.int32, (512, SN), 1)
     order = order_of(info, info[3] * 512, 0, (512, 1))
     c = [jnp.where(keep < info[4 + s], panel[:, SN * s:SN * s + SN], 0.0) for s in range(NSN)]
-    l0 = split(c[0])
-    l1 = split(c[1] - dot3(l0, got(6)))
-    l2 = split(c[2] - dot3(l0, got(7)) - dot3(l1, got(8)))
+    l0 = stack(c[0])
+    l1 = stack(c[1] - dot3(l0, got(6)))
+    l2 = stack(c[2] - dot3(l0, got(7)) - dot3(l1, got(8)))
+    live = jnp.concatenate([order, order], axis=0)
     for s, value in enumerate((l0, l1, l2)):
-        live = order > s
-        for part in range(2):
-            left[part, :, SN * s:SN * s + SN] = jnp.where(live, value[part], jnp.zeros_like(value[part]))
+        left[:, SN * s:SN * s + SN] = jnp.where(live > s, value, jnp.zeros_like(value))
 
 
 def update_kernel(info, front, *refs, second):
@@ -128,7 +132,7 @@
     step = pl.program_id(0)
 
     def got(n):
-        return blocks[2 * n], blocks[2 * n + 1]
+        return blocks[n, :SN], blocks[n, SN:]
 
     if second:
         left, _, out, quarter, band = refs[9:]
@@ -139,22 +143,21 @@
         def _():
             left_of(info, strips, got, left, panel)
 
-    place_rows(band, own, other, info)
+    half = info[8] if second else info[7]
     width = band.shape[1]
+    columns = pl.ds(pl.multiple_of(half * 512 + step * width, width), width)
+    place_rows(band, own, other, info, columns)
     keep = lax.broadcasted_iota(jnp.int32, (SN, width), 0)
     r = [jnp.where(keep < info[4 + s], band[SN * s:SN * s + SN, :], 0.0) for s in range(NSN)]
-    s0 = split(dot3(got(0), r[0]))
-    s1 = split(dot3(got(1), r[1] - dot3(got(3), s0)))
-    s2 = split(dot3(got(2), r[2] - dot3(got(4), s0) - dot3(got(5), s1)))
-    half = info[8] if second else info[7]
+    s0 = split(dot3(blocks[0], split(r[0])))
+    s1 = split(dot3(blocks[1], split(r[1] - dot3(blocks[3], s0))))
+    s2 = split(dot3(blocks[2], split(r[2] - dot3(blocks[4], s0) - dot3(blocks[5], s1))))
     order = order_of(info, info[2] * 1024 + half * 512 + step * width, 1, (1, width))
     total = None
     for s, value in enumerate((s0, s1, s2)):
         live = order > s
-        bh, bl = (jnp.where(live, part, jnp.zeros_like(part)) for part in value)
-        ah = left[0, :, SN * s:SN * s + SN]
-        al = left[1, :, SN * s:SN * s + SN]
-        term = mul(ah, bh) + (mul(ah, bl) + mul(al, bh))
+        masked = tuple(jnp.where(live, part, jnp.zeros_like(part)) for part in value)
+        term = dot3(left[:, SN * s:SN * s + SN], masked)
         total = term if total is None else total + term
     result = front[...] - total
     out[...] = result
@@ -163,6 +166,9 @@
             quarter[128 * i:128 * i + 128, 128 * j:128 * j + 128] = result[
                 256 * i + 128:256 * i + 256, 256 * j + 128:256 * j + 256
             ]
+
+
+VMEM_WHOLE = pl.BlockSpec(memory_space=pltpu.VMEM)
 
 
 def each(axis_size, target):
@@ -214,9 +220,9 @@
         pieces_kernel,
         grid_spec=pltpu.PrefetchScalarGridSpec(
             num_scalar_prefetch=1,
-            grid=(1,),
-            in_specs=[pl.BlockSpec((384, 1024), lambda i, info: (0, 0)), pl.BlockSpec((128, 1024), lambda i, info: (0, 0))],
-            out_specs=[pl.BlockSpec((48, 1024), lambda i, info: (0, 0))] * CHIPS,
+            grid=(),
+            in_specs=[VMEM_WHOLE] * 2,
+            out_specs=[VMEM_WHOLE] * CHIPS,
         ),
         out_shape=[jax.ShapeDtypeStruct((48, 1024), jnp.float32)] * CHIPS,
         name="pieces",
@@ -233,17 +239,16 @@
 
 
 def compute(info, matrix, band, pivot, strips):
-    vmem = pl.BlockSpec(memory_space=pltpu.VMEM)
     blocks = pl.pallas_call(
         factor_kernel,
         grid_spec=pltpu.PrefetchScalarGridSpec(
             num_scalar_prefetch=1,
             grid=(),
-            in_specs=[vmem] * 8,
-            out_specs=vmem,
+            in_specs=[VMEM_WHOLE] * 8,
+            out_specs=VMEM_WHOLE,
             scratch_shapes=[pltpu.VMEM((PIV, PIV), jnp.float32)],
         ),
-        out_shape=jax.ShapeDtypeStruct((18, SN, SN), jnp.bfloat16),
+        out_shape=jax.ShapeDtypeStruct((9, 2 * SN, SN), jnp.bfloat16),
         name="factor",
     )(info, *pivot[0], *pivot[1])
 
@@ -253,22 +258,18 @@
         def at(j, info):
             return (0, info[7 + which] * 2 + j)
 
-        whole = lambda shape: pl.BlockSpec(shape, lambda j, info: (0,) * len(shape))
-        left_shape = (2, 512, PIV)
-        if which:
-            specs = [whole(left_shape), pl.BlockSpec(memory_space=pl.ANY)]
-        else:
-            specs = [whole(value.shape) for value in inputs]
+        left_shape = (1024, PIV)
+        specs = [VMEM_WHOLE, pl.BlockSpec(memory_space=pl.ANY)] if which else [VMEM_WHOLE] * len(inputs)
         return pl.pallas_call(
             lambda *refs: update_kernel(*refs, second=which == 1),
             grid_spec=pltpu.PrefetchScalarGridSpec(
                 num_scalar_prefetch=1,
                 grid=(2,),
-                in_specs=[pl.BlockSpec((512, width), at)] + [pl.BlockSpec((96, width), at)] * 8 + [whole((18, SN, SN))] + specs,
+                in_specs=[pl.BlockSpec((512, width), at)] + [VMEM_WHOLE] * 9 + specs,
                 out_specs=[
                     pl.BlockSpec((512, width), at),
                     pl.BlockSpec((256, width // 2), lambda j, info: (0, j)),
-                ] + [whole(left_shape)] * (1 - which),
+                ] + [VMEM_WHOLE] * (1 - which),
                 scratch_shapes=[pltpu.VMEM((PIV, width), jnp.float32)] + [pltpu.VMEM((512, PIV), jnp.float32)] * (1 - which),
             ),
             out_shape=[

time: 148 us -> 149 us (level)
  no operation moved by 1% of the time
where the time goes in v1:
time: 149 us; the launch traced here: 148 us
  starting transfers between devices  72.9 us (49%)
  Pallas kernels  34.4 us (23%)
  waiting for transfers between devices  23.7 us (16%)
  other arithmetic  9.79 us (7%)
  local copies, waits for them, and re-layouts  6.36 us (4%)
    pallas_call x2, Pallas kernels, update(): pl.pallas_call(lambda *refs: update_kernel(*refs, second=which == 1), gri...  19.5 us
    ppermute x8, starting transfers between devices, gather_plane(): return (own, [lax.ppermute(part, 'row', CORE) for part in own])  14.6 us
    ppermute x3, starting transfers between devices, exchange(): lax.ppermute(panel[64 * z:64 * z + 128], 'col', [(0, z)])  14.3 us
    ppermute x7, starting transfers between devices, exchange(): lax.ppermute(pieces[q], 'row', [(0, 2 * q), (1, 2 * q + 1)])  13.7 us
    pallas_call x1, Pallas kernels, compute(): pl.pallas_call(factor_kernel, grid_spec=pltpu.PrefetchScalarGridSpec(num_...  11.4 us
    ppermute x3, waiting for transfers between devices, gather_line(): before.append(lax.ppermute(before[-1], 'col', Z_UP))  7.31 us
    ppermute x3, starting transfers between devices, exchange(): parts = [lax.ppermute(core_piece, 'col', [(0, z)]) for z in (4, 2, 6)]  6.78 us
    unnamed x68, local copies, waits for them, and re-layouts  4.85 us
  transfers between devices with their start and end apart: 43, of which 11 were waited for; matrix products, arithmetic and copies ran while one was open for 5% of the time, Pallas kernels for 14%

profile of v1, /device:TPU:1, one launch (start us, length us, event | category | flops | bytes accessed | tf_op | source)
XLA Modules:
  0.0 148.5 jit_solution(18387507523220828817)
XLA Ops:
  3.9 3.3 %bitcast_multiply_fusion.matrix.refs_1_ = f32[512,1024]{1,0:T(8,128)} fusion(f32[1,512,1024]{2,1,0:T(8,128)} %param.3, f32[4,1024]{1,0:T(4,128)S(1)} %bitcast.27), kind=kLoop, calls=%fused_computation | loop fusion | flops 524288 | bytes 4210688 | tf_op jit(solution)/shard_map/mul | solution.py:297
  9.3 3.5 %pieces.1 = (f32[48,1024]{1,0:T(8,128)}, f32[48,1024]{1,0:T(8,128)}, f32[48,1024]{1,0:T(8,128)}, f32[48,1024]{1,0:T(8,128)}, f32[48,1024]{1,0:T(8,128)}, /*index...) custom-call(s32[9]{0:T(128)} %concatenate.15.info.refs_0_, f32[512,1024]{1,0:T(8,128)} %bitcast_multiply_fusion.matrix.refs_1_, ...), custom_call_target="tpu_custom_call" | custom-call | tf_op jit(solution)/shard_map/pieces/pallas_call | solution.py:219
  12.8 4.6 %collective-permute-start.1 = (f32[48,1024]{1,0:T(8,128)}, f32[48,1024]{1,0:T(8,128)S(1)}, u32[]{:S(2)}, u32[]{:S(2)}) collective-permute-start(f32[48,1024]{1,0:T(8,128)} %get-tuple-element.16), channel_id=1, source_target_pairs={{0,32},{16,48},{1,33},{17,49},{2,34},{18,50},{3,35},{19,51},{4,36}... | collective-permute-start | bytes 589832 | tf_op jit(solution)/shard_map/ppermute | solution.py:230
  22.6 2.0 %collective-permute-start.6 = (f32[48,1024]{1,0:T(8,128)}, f32[48,1024]{1,0:T(8,128)}, u32[]{:S(2)}, u32[]{:S(2)}) collective-permute-start(f32[48,1024]{1,0:T(8,128)} %get-tuple-element.21), channel_id=1, source_target_pairs={{0,192},{16,208},{1,193},{17,209},{2,194},{18,210},{3,195},{19,211... | collective-permute-start | bytes 589832 | tf_op jit(solution)/shard_map/ppermute | solution.py:230
  25.3 2.0 %collective-permute-start.7 = (f32[48,1024]{1,0:T(8,128)}, f32[48,1024]{1,0:T(8,128)}, u32[]{:S(2)}, u32[]{:S(2)}) collective-permute-start(f32[48,1024]{1,0:T(8,128)} %get-tuple-element.22), channel_id=1, source_target_pairs={{0,224},{16,240},{1,225},{17,241},{2,226},{18,242},{3,227},{19,243... | collective-permute-start | bytes 589832 | tf_op jit(solution)/shard_map/ppermute | solution.py:230
  27.3 9.6 %collective-permute-start.31 = (f32[128,768]{1,0:T(8,128)S(1)}, f32[128,768]{1,0:T(8,128)}, u32[]{:S(2)}, u32[]{:S(2)}) collective-permute-start(f32[128,768]{1,0:T(8,128)S(1)} %get-tuple-element.28), channel_id=1, source_target_pairs={{0,8},{1,9},{16,24},{17,25},{32,40},{33,41},{48,56},{49,57},{64,72... | collective-permute-start | bytes 1179656 | tf_op jit(solution)/shard_map/ppermute | solution.py:215
  36.9 2.7 %collective-permute-start.32 = (f32[128,768]{1,0:T(8,128)S(1)}, f32[128,768]{1,0:T(8,128)}, u32[]{:S(2)}, u32[]{:S(2)}) collective-permute-start(f32[128,768]{1,0:T(8,128)S(1)} %get-tuple-element.29), channel_id=1, source_target_pairs={{0,12},{1,13},{16,28},{17,29},{32,44},{33,45},{48,60},{49,61},{64,... | collective-permute-start | bytes 1179656 | tf_op jit(solution)/shard_map/ppermute | solution.py:215
  40.3 2.0 %collective-permute-start.30 = (f32[128,768]{1,0:T(8,128)S(1)}, f32[128,768]{1,0:T(8,128)}, u32[]{:S(2)}, u32[]{:S(2)}) collective-permute-start(f32[128,768]{1,0:T(8,128)S(1)} %get-tuple-element.30), channel_id=1, source_target_pairs={{0,4},{1,5},{16,20},{17,21},{32,36},{33,37},{48,52},{49,53},{64,68... | collective-permute-start | bytes 1179656 | tf_op jit(solution)/shard_map/ppermute | solution.py:215
  42.4 1.5 %add_select_fusion = f32[48,1024]{1,0:T(8,128)S(1)} fusion(f32[48,1024]{1,0:T(8,128)S(1)} %copy-done.20, f32[48,1024]{1,0:T(8,128)} %collective-permute-done.7, f32[48,1024]{1,0:T(8,128)} %collective-permute-done.6, f32[48,1024]{1,0:T(8,128)} %copy-done.25, f32[48,1024]{1,0:T(8,128)} %copy-done.24, f32[48,1024]{1,0:T(8,128)} %copy-done.23, ...), kind=kLoop, calls=%fused_computation.7 | loop fusion | flops 344064 | bytes 1769473 | tf_op jit(solution)/shard_map/jit(_where)/select_n | solution.py:231
  43.9 2.8 %collective-permute-start.19 = (f32[48,768]{1,0:T(8,128)S(1)}, f32[48,768]{1,0:T(8,128)S(1)}, u32[]{:S(2)}, u32[]{:S(2)}) collective-permute-start(f32[48,768]{1,0:T(8,128)S(1)} %slice.69), channel_id=1, source_target_pairs={{0,12},{1,13},{16,28},{17,29},{32,44},{33,45},{48,60},{49,61},{64,... | collective-permute-start | bytes 442376 | tf_op jit(solution)/shard_map/ppermute | solution.py:234
  48.0 2.6 %collective-permute-start.17 = (f32[48,768]{1,0:T(8,128)S(1)}, f32[48,768]{1,0:T(8,128)S(1)}, u32[]{:S(2)}, u32[]{:S(2)}) collective-permute-start(f32[48,768]{1,0:T(8,128)S(1)} %slice.69), channel_id=1, source_target_pairs={{0,8},{1,9},{16,24},{17,25},{32,40},{33,41},{48,56},{49,57},{64,72... | collective-permute-start | bytes 442376 | tf_op jit(solution)/shard_map/ppermute | solution.py:234
  54.2 3.2 %collective-permute-done.17 = f32[48,768]{1,0:T(8,128)S(1)} collective-permute-done((f32[48,768]{1,0:T(8,128)S(1)}, f32[48,768]{1,0:T(8,128)S(1)}, u32[]{:S(2)}, u32[]{:S(2)}) %collective-permute-start.17) | collective-permute-done | bytes 147488 | tf_op jit(solution)/shard_map/ppermute | solution.py:234
  58.7 2.9 %collective-permute-done.33 = f32[64,768]{1,0:T(8,128)S(1)} collective-permute-done((f32[64,768]{1,0:T(8,128)S(1)}, f32[64,768]{1,0:T(8,128)S(1)}, u32[]{:S(2)}, u32[]{:S(2)}) %collective-permute-start.33) | collective-permute-done | bytes 196640 | tf_op jit(solution)/shard_map/ppermute | solution.py:217
  61.6 2.0 %collective-permute-start.37 = (f32[64,768]{1,0:T(8,128)S(1)}, f32[64,768]{1,0:T(8,128)S(1)}, u32[]{:S(2)}, u32[]{:S(2)}) collective-permute-start(f32[64,768]{1,0:T(8,128)S(1)} %slice_select_fusion.1.refs_11_), channel_id=1, source_target_pairs={{0,2},{2,4},{4,6},{6,8},{8,10},{10,12},{12,14},{14,0},{1,3},{3,5},... | collective-permute-start | bytes 589832 | tf_op jit(solution)/shard_map/ppermute | solution.py:203
  63.6 1.8 %collective-permute-start.8 = (f32[48,1024]{1,0:T(8,128)S(1)}, f32[48,1024]{1,0:T(8,128)S(1)}, u32[]{:S(2)}, u32[]{:S(2)}) collective-permute-start(f32[48,1024]{1,0:T(8,128)S(1)} %add_select_fusion), channel_id=1, source_target_pairs={{0,32},{16,48},{32,0},{48,16},{64,96},{80,112},{96,64},{112,80},{1... | collective-permute-start | bytes 589832 | tf_op jit(solution)/shard_map/ppermute | solution.py:189
  66.6 2.9 %collective-permute-done.8 = f32[48,1024]{1,0:T(8,128)S(1)} collective-permute-done((f32[48,1024]{1,0:T(8,128)S(1)}, f32[48,1024]{1,0:T(8,128)S(1)}, u32[]{:S(2)}, u32[]{:S(2)}) %collective-permute-start.8) | collective-permute-done | bytes 196640 | tf_op jit(solution)/shard_map/ppermute | solution.py:189
  71.8 2.1 %collective-permute-start.9 = (f32[96,1024]{1,0:T(8,128)S(1)}, f32[96,1024]{1,0:T(8,128)S(1)}, u32[]{:S(2)}, u32[]{:S(2)}) collective-permute-start(f32[96,1024]{1,0:T(8,128)S(1)} %pad_maximum_fusion.refs_2_), channel_id=1, source_target_pairs={{0,192},{16,208},{32,224},{48,240},{64,0},{80,16},{96,32},{112,48}... | collective-permute-start | bytes 1179656 | tf_op jit(solution)/shard_map/ppermute | solution.py:192
  74.1 3.1 %collective-permute-done.38.refs_18_ = f32[64,768]{1,0:T(8,128)S(1)} collective-permute-done((f32[64,768]{1,0:T(8,128)S(1)}, f32[64,768]{1,0:T(8,128)S(1)}, u32[]{:S(2)}, u32[]{:S(2)}) %collective-permute-start.38) | collective-permute-done | bytes 196640 | tf_op jit(solution)/shard_map/ppermute | solution.py:203
  77.1 1.8 %collective-permute-start.22 = (f32[96,768]{1,0:T(8,128)S(1)}, f32[96,768]{1,0:T(8,128)S(1)}, u32[]{:S(2)}, u32[]{:S(2)}) collective-permute-start(f32[96,768]{1,0:T(8,128)S(1)} %pad_maximum_fusion.1.refs_0_), channel_id=1, source_target_pairs={{0,192},{16,208},{32,224},{48,240},{64,0},{80,16},{96,32},{112,48}... | collective-permute-start | bytes 884744 | tf_op jit(solution)/shard_map/ppermute | solution.py:192
  79.1 2.7 %collective-permute-start.35 = (f32[64,768]{1,0:T(8,128)S(1)}, f32[64,768]{1,0:T(8,128)S(1)}, u32[]{:S(2)}, u32[]{:S(2)}) collective-permute-start(f32[64,768]{1,0:T(8,128)S(1)} %collective-permute-done.34.refs_12_), channel_id=1, source_target_pairs={{0,14},{2,0},{4,2},{6,4},{8,6},{10,8},{12,10},{14,12},{1,15},{3,1}... | collective-permute-start | bytes 589832 | tf_op jit(solution)/shard_map/ppermute | solution.py:204
  81.9 4.2 %collective-permute-done.39.refs_17_ = f32[64,768]{1,0:T(8,128)S(1)} collective-permute-done((f32[64,768]{1,0:T(8,128)S(1)}, f32[64,768]{1,0:T(8,128)S(1)}, u32[]{:S(2)}, u32[]{:S(2)}) %collective-permute-start.39) | collective-permute-done | bytes 196640 | tf_op jit(solution)/shard_map/ppermute | solution.py:203
  86.1 9.5 %collective-permute-start.26 = (f32[96,768]{1,0:T(8,128)S(1)}, f32[96,768]{1,0:T(8,128)}, u32[]{:S(2)}, u32[]{:S(2)}) collective-permute-start(f32[96,768]{1,0:T(8,128)S(1)} %pad_maximum_fusion.1.refs_0_), channel_id=1, source_target_pairs={{0,16},{16,0},{32,48},{48,32},{64,80},{80,64},{96,112},{112,96},{1... | collective-permute-start | bytes 884744 | tf_op jit(solution)/shard_map/ppermute | solution.py:196
  95.7 1.3 collective-permute-start.24
  97.0 1.5 %collective-permute-start.25 = (f32[48,768]{1,0:T(8,128)S(1)}, f32[48,768]{1,0:T(8,128)S(1)}, u32[]{:S(2)}, u32[]{:S(2)}) collective-permute-start(f32[48,768]{1,0:T(8,128)S(1)} %slice.71), channel_id=1, source_target_pairs={{0,192},{16,208},{32,224},{48,240},{64,0},{80,16},{96,32},{112,48}... | collective-permute-start | bytes 442376 | tf_op jit(solution)/shard_map/ppermute | solution.py:194
  99.2 1.6 %collective-permute-start.27 = (f32[96,768]{1,0:T(8,128)S(1)}, f32[96,768]{1,0:T(8,128)S(1)}, u32[]{:S(2)}, u32[]{:S(2)}) collective-permute-start(f32[96,768]{1,0:T(8,128)S(1)} %collective-permute-done.22.refs_1_), channel_id=1, source_target_pairs={{0,16},{16,0},{32,48},{48,32},{64,80},{80,64},{96,112},{112,96},{1... | collective-permute-start | bytes 884744 | tf_op jit(solution)/shard_map/ppermute | solution.py:196
  100.8 1.5 %collective-permute-done.24 = f32[48,768]{1,0:T(8,128)S(1)} collective-permute-done((f32[48,768]{1,0:T(8,128)S(1)}, f32[48,768]{1,0:T(8,128)S(1)}, u32[]{:S(2)}, u32[]{:S(2)}) %collective-permute-start.24) | collective-permute-done | bytes 147488 | tf_op jit(solution)/shard_map/ppermute | solution.py:193
  103.9 4.0 %collective-permute-done.36.refs_14_ = f32[64,768]{1,0:T(8,128)S(1)} collective-permute-done((f32[64,768]{1,0:T(8,128)S(1)}, f32[64,768]{1,0:T(8,128)S(1)}, u32[]{:S(2)}, u32[]{:S(2)}) %collective-permute-start.36) | collective-permute-done | bytes 196640 | tf_op jit(solution)/shard_map/ppermute | solution.py:204
  107.9 1.7 %collective-permute-start.13 = (f32[96,1024]{1,0:T(8,128)S(1)}, f32[96,1024]{1,0:T(8,128)S(1)}, u32[]{:S(2)}, u32[]{:S(2)}) collective-permute-start(f32[96,1024]{1,0:T(8,128)S(1)} %pad_maximum_fusion.refs_2_), channel_id=1, source_target_pairs={{0,16},{16,0},{32,48},{48,32},{64,80},{80,64},{96,112},{112,96},{1... | collective-permute-start | bytes 1179656 | tf_op jit(solution)/shard_map/ppermute | solution.py:196
  113.5 11.4 %factor.1.refs_10_ = bf16[9,512,256]{2,1,0:T(8,128)(2,1)} custom-call(s32[9]{0:T(128)} %concatenate.15.info.refs_0_, f32[96,768]{1,0:T(8,128)} %copy-done.9, f32[96,768]{1,0:T(8,128)} %copy-done.12, f32[96,768]{1,0:T(8,128)} %copy-done.13, f32[96,768]{1,0:T(8,128)} %copy-done.11, f32[96,768]{1,0:T(8,128)} %collective-permute-done.26.refs_4_, ...), custom_call_target="tpu_custom_call" | custom-call | tf_op jit(solution)/shard_map/factor/pallas_call | solution.py:242
  126.8 10.2 %update.2 = (f32[512,1024]{1,0:T(8,128)}, f32[256,256]{1,0:T(8,128)}, bf16[1024,768]{1,0:T(8,128)(2,1)}) custom-call(s32[9]{0:T(128)} %concatenate.15.info.refs_0_, f32[512,1024]{1,0:T(8,128)} %bitcast_multiply_fusion.matrix.refs_1_, f32[96,1024]{1,0:T(8,128)} %copy-done.1, f32[96,1024]{1,0:T(8,128)} %copy-done.3, f32[96,1024]{1,0:T(8,128)} %copy-done.4, ...), custom_call_target="tpu_custom_call" | custom-call | tf_op jit(solution)/shard_map/update/pallas_call | solution.py:263
  137.5 9.3 %update.3 = (f32[512,1024]{1,0:T(8,128)}, f32[256,256]{1,0:T(8,128)}) custom-call(s32[9]{0:T(128)} %concatenate.15.info.refs_0_, f32[512,1024]{1,0:T(8,128)} %bitcast_multiply_fusion.matrix.refs_1_, f32[96,1024]{1,0:T(8,128)} %copy-done.1, f32[96,1024]{1,0:T(8,128)} %copy-done.3, f32[96,1024]{1,0:T(8,128)} %copy-done.4, ...), custom_call_target="tpu_custom_call", output_to_operand_aliasing={{0}: (12, {})} | custom-call | tf_op jit(solution)/shard_map/update/pallas_call | solution.py:263
  146.8 1.7 %add.82 = f32[256,256]{1,0:T(8,128)} add(f32[256,256]{1,0:T(8,128)} %get-tuple-element.26, f32[256,256]{1,0:T(8,128)S(1)} %collective-permute-done.42) | non-fusion elementwise | flops 65536 | bytes 786432 | tf_op jit(solution)/shard_map/add | solution.py:286
  (154 shorter events, 30.3 us)
Async XLA Ops:
  12.8 9.8 %collective-permute-start.1 = (f32[48,1024]{1,0:T(8,128)}, f32[48,1024]{1,0:T(8,128)S(1)}, u32[]{:S(2)}, u32[]{:S(2)}) collective-permute-start(f32[48,1024]{1,0:T(8,128)} %get-tuple-element.16), channel_id=1, source_target_pairs={{0,32},{16,48},{1,33},{17,49},{2,34},{18,50},{3,35},{19,51},{4,36}... | collective-permute-start | bytes 589832 | tf_op jit(solution)/shard_map/ppermute | solution.py:230
  18.7 8.7 %collective-permute-start.3 = (f32[48,1024]{1,0:T(8,128)}, f32[48,1024]{1,0:T(8,128)S(1)}, u32[]{:S(2)}, u32[]{:S(2)}) collective-permute-start(f32[48,1024]{1,0:T(8,128)} %get-tuple-element.18), channel_id=1, source_target_pairs={{0,96},{16,112},{1,97},{17,113},{2,98},{18,114},{3,99},{19,115},{4... | collective-permute-start | bytes 589832 | tf_op jit(solution)/shard_map/ppermute | solution.py:230
  20.0 17.0 %collective-permute-start.4 = (f32[48,1024]{1,0:T(8,128)}, f32[48,1024]{1,0:T(8,128)S(1)}, u32[]{:S(2)}, u32[]{:S(2)}) collective-permute-start(f32[48,1024]{1,0:T(8,128)} %get-tuple-element.19), channel_id=1, source_target_pairs={{0,128},{16,144},{1,129},{17,145},{2,130},{18,146},{3,131},{19,147... | collective-permute-start | bytes 589832 | tf_op jit(solution)/shard_map/ppermute | solution.py:230
  21.3 18.4 %collective-permute-start.5 = (f32[48,1024]{1,0:T(8,128)}, f32[48,1024]{1,0:T(8,128)S(1)}, u32[]{:S(2)}, u32[]{:S(2)}) collective-permute-start(f32[48,1024]{1,0:T(8,128)} %get-tuple-element.20), channel_id=1, source_target_pairs={{0,160},{16,176},{1,161},{17,177},{2,162},{18,178},{3,163},{19,179... | collective-permute-start | bytes 589832 | tf_op jit(solution)/shard_map/ppermute | solution.py:230
  22.6 19.8 %collective-permute-start.6 = (f32[48,1024]{1,0:T(8,128)}, f32[48,1024]{1,0:T(8,128)}, u32[]{:S(2)}, u32[]{:S(2)}) collective-permute-start(f32[48,1024]{1,0:T(8,128)} %get-tuple-element.21), channel_id=1, source_target_pairs={{0,192},{16,208},{1,193},{17,209},{2,194},{18,210},{3,195},{19,211... | collective-permute-start | bytes 589832 | tf_op jit(solution)/shard_map/ppermute | solution.py:230
  25.3 17.1 %collective-permute-start.7 = (f32[48,1024]{1,0:T(8,128)}, f32[48,1024]{1,0:T(8,128)}, u32[]{:S(2)}, u32[]{:S(2)}) collective-permute-start(f32[48,1024]{1,0:T(8,128)} %get-tuple-element.22), channel_id=1, source_target_pairs={{0,224},{16,240},{1,225},{17,241},{2,226},{18,242},{3,227},{19,243... | collective-permute-start | bytes 589832 | tf_op jit(solution)/shard_map/ppermute | solution.py:230
  27.3 20.7 %collective-permute-start.31 = (f32[128,768]{1,0:T(8,128)S(1)}, f32[128,768]{1,0:T(8,128)}, u32[]{:S(2)}, u32[]{:S(2)}) collective-permute-start(f32[128,768]{1,0:T(8,128)S(1)} %get-tuple-element.28), channel_id=1, source_target_pairs={{0,8},{1,9},{16,24},{17,25},{32,40},{33,41},{48,56},{49,57},{64,72... | collective-permute-start | bytes 1179656 | tf_op jit(solution)/shard_map/ppermute | solution.py:215
  36.9 13.8 %collective-permute-start.32 = (f32[128,768]{1,0:T(8,128)S(1)}, f32[128,768]{1,0:T(8,128)}, u32[]{:S(2)}, u32[]{:S(2)}) collective-permute-start(f32[128,768]{1,0:T(8,128)S(1)} %get-tuple-element.29), channel_id=1, source_target_pairs={{0,12},{1,13},{16,28},{17,29},{32,44},{33,45},{48,60},{49,61},{64,... | collective-permute-start | bytes 1179656 | tf_op jit(solution)/shard_map/ppermute | solution.py:215
  40.3 10.7 %collective-permute-start.30 = (f32[128,768]{1,0:T(8,128)S(1)}, f32[128,768]{1,0:T(8,128)}, u32[]{:S(2)}, u32[]{:S(2)}) collective-permute-start(f32[128,768]{1,0:T(8,128)S(1)} %get-tuple-element.30), channel_id=1, source_target_pairs={{0,4},{1,5},{16,20},{17,21},{32,36},{33,37},{48,52},{49,53},{64,68... | collective-permute-start | bytes 1179656 | tf_op jit(solution)/shard_map/ppermute | solution.py:215
  43.9 9.8 %collective-permute-start.19 = (f32[48,768]{1,0:T(8,128)S(1)}, f32[48,768]{1,0:T(8,128)S(1)}, u32[]{:S(2)}, u32[]{:S(2)}) collective-permute-start(f32[48,768]{1,0:T(8,128)S(1)} %slice.69), channel_id=1, source_target_pairs={{0,12},{1,13},{16,28},{17,29},{32,44},{33,45},{48,60},{49,61},{64,... | collective-permute-start | bytes 442376 | tf_op jit(solution)/shard_map/ppermute | solution.py:234
  46.7 7.4 %collective-permute-start.18 = (f32[48,768]{1,0:T(8,128)S(1)}, f32[48,768]{1,0:T(8,128)S(1)}, u32[]{:S(2)}, u32[]{:S(2)}) collective-permute-start(f32[48,768]{1,0:T(8,128)S(1)} %slice.69), channel_id=1, source_target_pairs={{0,4},{1,5},{16,20},{17,21},{32,36},{33,37},{48,52},{49,53},{64,68... | collective-permute-start | bytes 442376 | tf_op jit(solution)/shard_map/ppermute | solution.py:234
  48.0 9.3 %collective-permute-start.17 = (f32[48,768]{1,0:T(8,128)S(1)}, f32[48,768]{1,0:T(8,128)S(1)}, u32[]{:S(2)}, u32[]{:S(2)}) collective-permute-start(f32[48,768]{1,0:T(8,128)S(1)} %slice.69), channel_id=1, source_target_pairs={{0,8},{1,9},{16,24},{17,25},{32,40},{33,41},{48,56},{49,57},{64,72... | collective-permute-start | bytes 442376 | tf_op jit(solution)/shard_map/ppermute | solution.py:234
  52.3 9.2 %collective-permute-start.33 = (f32[64,768]{1,0:T(8,128)S(1)}, f32[64,768]{1,0:T(8,128)S(1)}, u32[]{:S(2)}, u32[]{:S(2)}) collective-permute-start(f32[64,768]{1,0:T(8,128)S(1)} %slice.76), channel_id=1, source_target_pairs={{0,2},{4,6},{8,10},{12,14},{1,3},{5,7},{9,11},{13,15},{16,18},{20,... | collective-permute-start | bytes 589832 | tf_op jit(solution)/shard_map/ppermute | solution.py:217
  57.4 8.0 %collective-permute-start.20 = (f32[48,768]{1,0:T(8,128)S(1)}, f32[48,768]{1,0:T(8,128)S(1)}, u32[]{:S(2)}, u32[]{:S(2)}) collective-permute-start(f32[48,768]{1,0:T(8,128)S(1)} %add_select_fusion.1), channel_id=1, source_target_pairs={{0,2},{4,6},{8,10},{12,14},{1,3},{5,7},{9,11},{13,15},{16,18},{20,... | collective-permute-start | bytes 442376 | tf_op jit(solution)/shard_map/ppermute | solution.py:236
  61.6 9.5 %collective-permute-start.37 = (f32[64,768]{1,0:T(8,128)S(1)}, f32[64,768]{1,0:T(8,128)S(1)}, u32[]{:S(2)}, u32[]{:S(2)}) collective-permute-start(f32[64,768]{1,0:T(8,128)S(1)} %slice_select_fusion.1.refs_11_), channel_id=1, source_target_pairs={{0,2},{2,4},{4,6},{6,8},{8,10},{10,12},{12,14},{14,0},{1,3},{3,5},... | collective-permute-start | bytes 589832 | tf_op jit(solution)/shard_map/ppermute | solution.py:203
  65.3 8.6 %collective-permute-start.21 = (f32[48,768]{1,0:T(8,128)S(1)}, f32[48,768]{1,0:T(8,128)S(1)}, u32[]{:S(2)}, u32[]{:S(2)}) collective-permute-start(f32[48,768]{1,0:T(8,128)S(1)} %broadcast_select_fusion.2), channel_id=1, source_target_pairs={{0,32},{16,48},{32,0},{48,16},{64,96},{80,112},{96,64},{112,80},{1... | collective-permute-start | bytes 442376 | tf_op jit(solution)/shard_map/ppermute | solution.py:189
  69.7 9.3 %collective-permute-start.10 = (f32[96,1024]{1,0:T(8,128)S(1)}, f32[96,1024]{1,0:T(8,128)S(1)}, u32[]{:S(2)}, u32[]{:S(2)}) collective-permute-start(f32[96,1024]{1,0:T(8,128)S(1)} %pad_maximum_fusion.refs_2_), channel_id=1, source_target_pairs={{0,64},{16,80},{32,96},{48,112},{64,128},{80,144},{96,160},{112,17... | collective-permute-start | bytes 1179656 | tf_op jit(solution)/shard_map/ppermute | solution.py:191
  70.3 8.6 %collective-permute-start.34 = (f32[64,768]{1,0:T(8,128)S(1)}, f32[64,768]{1,0:T(8,128)S(1)}, u32[]{:S(2)}, u32[]{:S(2)}) collective-permute-start(f32[64,768]{1,0:T(8,128)S(1)} %slice_select_fusion.1.refs_11_), channel_id=1, source_target_pairs={{0,14},{2,0},{4,2},{6,4},{8,6},{10,8},{12,10},{14,12},{1,15},{3,1}... | collective-permute-start | bytes 589832 | tf_op jit(solution)/shard_map/ppermute | solution.py:204
  74.0 12.2 %collective-permute-start.23 = (f32[96,768]{1,0:T(8,128)S(1)}, f32[96,768]{1,0:T(8,128)S(1)}, u32[]{:S(2)}, u32[]{:S(2)}) collective-permute-start(f32[96,768]{1,0:T(8,128)S(1)} %pad_maximum_fusion.1.refs_0_), channel_id=1, source_target_pairs={{0,64},{16,80},{32,96},{48,112},{64,128},{80,144},{96,160},{112,17... | collective-permute-start | bytes 884744 | tf_op jit(solution)/shard_map/ppermute | solution.py:191
  77.1 18.5 %collective-permute-start.22 = (f32[96,768]{1,0:T(8,128)S(1)}, f32[96,768]{1,0:T(8,128)S(1)}, u32[]{:S(2)}, u32[]{:S(2)}) collective-permute-start(f32[96,768]{1,0:T(8,128)S(1)} %pad_maximum_fusion.1.refs_0_), channel_id=1, source_target_pairs={{0,192},{16,208},{32,224},{48,240},{64,0},{80,16},{96,32},{112,48}... | collective-permute-start | bytes 884744 | tf_op jit(solution)/shard_map/ppermute | solution.py:192
  79.0 18.0 %collective-permute-start.11 = (f32[48,1024]{1,0:T(8,128)S(1)}, f32[48,1024]{1,0:T(8,128)S(1)}, u32[]{:S(2)}, u32[]{:S(2)}) collective-permute-start(f32[48,1024]{1,0:T(8,128)S(1)} %slice.67), channel_id=1, source_target_pairs={{0,64},{16,80},{32,96},{48,112},{64,128},{80,144},{96,160},{112,17... | collective-permute-start | bytes 589832 | tf_op jit(solution)/shard_map/ppermute | solution.py:193
  79.1 19.5 %collective-permute-start.35 = (f32[64,768]{1,0:T(8,128)S(1)}, f32[64,768]{1,0:T(8,128)S(1)}, u32[]{:S(2)}, u32[]{:S(2)}) collective-permute-start(f32[64,768]{1,0:T(8,128)S(1)} %collective-permute-done.34.refs_12_), channel_id=1, source_target_pairs={{0,14},{2,0},{4,2},{6,4},{8,6},{10,8},{12,10},{14,12},{1,15},{3,1}... | collective-permute-start | bytes 589832 | tf_op jit(solution)/shard_map/ppermute | solution.py:204
  86.1 13.1 %collective-permute-start.12 = (f32[48,1024]{1,0:T(8,128)S(1)}, f32[48,1024]{1,0:T(8,128)S(1)}, u32[]{:S(2)}, u32[]{:S(2)}) collective-permute-start(f32[48,1024]{1,0:T(8,128)S(1)} %slice.68), channel_id=1, source_target_pairs={{0,192},{16,208},{32,224},{48,240},{64,0},{80,16},{96,32},{112,48}... | collective-permute-start | bytes 589832 | tf_op jit(solution)/shard_map/ppermute | solution.py:194
  86.1 23.6 %collective-permute-start.26 = (f32[96,768]{1,0:T(8,128)S(1)}, f32[96,768]{1,0:T(8,128)}, u32[]{:S(2)}, u32[]{:S(2)}) collective-permute-start(f32[96,768]{1,0:T(8,128)S(1)} %pad_maximum_fusion.1.refs_0_), channel_id=1, source_target_pairs={{0,16},{16,0},{32,48},{48,32},{64,80},{80,64},{96,112},{112,96},{1... | collective-permute-start | bytes 884744 | tf_op jit(solution)/shard_map/ppermute | solution.py:196
  98.6 11.6 %collective-permute-start.29 = (f32[96,768]{1,0:T(8,128)S(1)}, f32[96,768]{1,0:T(8,128)S(1)}, u32[]{:S(2)}, u32[]{:S(2)}) collective-permute-start(f32[96,768]{1,0:T(8,128)S(1)} %collective-permute-done.23.refs_3_), channel_id=1, source_target_pairs={{0,16},{16,0},{32,48},{48,32},{64,80},{80,64},{96,112},{112,96},{1... | collective-permute-start | bytes 884744 | tf_op jit(solution)/shard_map/ppermute | solution.py:196
  99.2 11.1 %collective-permute-start.27 = (f32[96,768]{1,0:T(8,128)S(1)}, f32[96,768]{1,0:T(8,128)S(1)}, u32[]{:S(2)}, u32[]{:S(2)}) collective-permute-start(f32[96,768]{1,0:T(8,128)S(1)} %collective-permute-done.22.refs_1_), channel_id=1, source_target_pairs={{0,16},{16,0},{32,48},{48,32},{64,80},{80,64},{96,112},{112,96},{1... | collective-permute-start | bytes 884744 | tf_op jit(solution)/shard_map/ppermute | solution.py:196
  107.9 17.0 %collective-permute-start.13 = (f32[96,1024]{1,0:T(8,128)S(1)}, f32[96,1024]{1,0:T(8,128)S(1)}, u32[]{:S(2)}, u32[]{:S(2)}) collective-permute-start(f32[96,1024]{1,0:T(8,128)S(1)} %pad_maximum_fusion.refs_2_), channel_id=1, source_target_pairs={{0,16},{16,0},{32,48},{48,32},{64,80},{80,64},{96,112},{112,96},{1... | collective-permute-start | bytes 1179656 | tf_op jit(solution)/shard_map/ppermute | solution.py:196
  109.8 15.2 %collective-permute-start.16 = (f32[96,1024]{1,0:T(8,128)S(1)}, f32[96,1024]{1,0:T(8,128)S(1)}, u32[]{:S(2)}, u32[]{:S(2)}) collective-permute-start(f32[96,1024]{1,0:T(8,128)S(1)} %collective-permute-done.10.refs_5_), channel_id=1, source_target_pairs={{0,16},{16,0},{32,48},{48,32},{64,80},{80,64},{96,112},{112,96},{1... | collective-permute-start | bytes 1179656 | tf_op jit(solution)/shard_map/ppermute | solution.py:196
  110.2 14.8 %collective-permute-start.14 = (f32[96,1024]{1,0:T(8,128)S(1)}, f32[96,1024]{1,0:T(8,128)S(1)}, u32[]{:S(2)}, u32[]{:S(2)}) collective-permute-start(f32[96,1024]{1,0:T(8,128)S(1)} %collective-permute-done.9.refs_3_), channel_id=1, source_target_pairs={{0,16},{16,0},{32,48},{48,32},{64,80},{80,64},{96,112},{112,96},{1... | collective-permute-start | bytes 1179656 | tf_op jit(solution)/shard_map/ppermute | solution.py:196
  110.4 14.7 %collective-permute-start.15 = (f32[96,1024]{1,0:T(8,128)S(1)}, f32[96,1024]{1,0:T(8,128)S(1)}, u32[]{:S(2)}, u32[]{:S(2)}) collective-permute-start(f32[96,1024]{1,0:T(8,128)S(1)} %constant_dynamic-update-slice_fusion.refs_4_), channel_id=1, source_target_pairs={{0,16},{16,0},{32,48},{48,32},{64,80},{80,64},{96,112},{112,96},{1... | collective-permute-start | bytes 1179656 | tf_op jit(solution)/shard_map/ppermute | solution.py:196
  112.3 12.6 %collective-permute-start.41 = (f32[32,768]{1,0:T(8,128)}, f32[32,768]{1,0:T(8,128)}, u32[]{:S(2)}, u32[]{:S(2)}) collective-permute-start(f32[32,768]{1,0:T(8,128)} %slice.79), channel_id=1, source_target_pairs={{0,14},{2,0},{4,2},{6,4},{8,6},{10,8},{12,10},{14,12},{1,15},{3,1}... | collective-permute-start | bytes 294920 | tf_op jit(solution)/shard_map/ppermute | solution.py:206
  137.0 9.8 %collective-permute-start.42 = (f32[256,256]{1,0:T(8,128)}, f32[256,256]{1,0:T(8,128)S(1)}, u32[]{:S(2)}, u32[]{:S(2)}) collective-permute-start(f32[256,256]{1,0:T(8,128)} %get-tuple-element.27), channel_id=1, source_target_pairs={{0,1},{1,0},{2,3},{3,2},{4,5},{5,4},{6,7},{7,6},{8,9},{9,8},{10,11... | collective-permute-start | bytes 786440 | tf_op jit(solution)/shard_map/ppermute | solution.py:284
  (43 other events, 543.8 us)

commit v2 on v1

--- a/solution.py
+++ b/solution.py
@@ -61,16 +61,31 @@
                 target[pl.ds(pl.multiple_of(256 + 128 * c + 16 * chip, 16), 16), :] = parts[k][48 * e + 32:48 * e + 48, columns]
 
 
-def pieces_kernel(info, matrix, moved, *out):
+def pieces_kernel(info, front, kept, moved, *out):
     first = info[1] == 0
     for q in range(CHIPS):
-        out[q][:32, :] = matrix[32 * q:32 * q + 32, :]
-        mine = matrix[256 + 16 * q:272 + 16 * q, :]
-        out[q][32:, :] = jnp.where(first, mine, moved[16 * q:16 * q + 16, :])
-
-
-def factor_kernel(info, *refs):
-    out, matrix = refs[8:]
+        high = front[32 * q:32 * q + 32, :] * kept[q // 4:q // 4 + 1, :]
+        mine = front[256 + 16 * q:272 + 16 * q, :] * kept[2:3, :]
+        low = jnp.where(first, mine, moved[16 * q:16 * q + 16, :])
+        for target in (out[q], out[CHIPS + q]):
+            width = target.shape[1]
+            target[:32, :] = high[:, :width]
+            target[32:, :] = low[:, :width]
+
+
+def with_ones(info, value, i):
+    row_ids = lax.broadcasted_iota(jnp.int32, (SN, SN), 0)
+    col_ids = lax.broadcasted_iota(jnp.int32, (SN, SN), 1)
+    return jnp.where((row_ids == col_ids) & (row_ids >= info[4 + i]), 1.0, value)
+
+
+def put_pair(target, pair):
+    target[:SN] = pair[0]
+    target[SN:] = pair[1]
+
+
+def factor_first(info, *refs):
+    done, rest, matrix = refs[8:]
     place_rows(matrix, refs[:4], refs[4:8], info)
     row_ids = lax.broadcasted_iota(jnp.int32, (SN, SN), 0)
     col_ids = lax.broadcasted_iota(jnp.int32, (SN, SN), 1)
@@ -79,24 +94,34 @@
         keep = (row_ids < info[4 + i]) & (col_ids < info[4 + j])
         return jnp.where(keep, matrix[SN * i:SN * i + SN, SN * j:SN * j + SN], 0.0)
 
-    def pivot(value, i):
-        return jnp.where((row_ids == col_ids) & (row_ids >= info[4 + i]), 1.0, value)
-
-    i0 = stack(inverse(pivot(block(0, 0), 0)))
+    i0 = stack(inverse(with_ones(info, block(0, 0), 0)))
     v01 = split(dot3(i0, split(block(0, 1))))
     v02 = split(dot3(i0, split(block(0, 2))))
     m10 = stack(block(1, 0))
     m20 = stack(block(2, 0))
-    i1 = stack(inverse(pivot(block(1, 1) - dot3(m10, v01), 1)))
-    m12 = block(1, 2) - dot3(m10, v02)
-    m21 = stack(block(2, 1) - dot3(m20, v01))
-    v12 = split(dot3(i1, split(m12)))
-    i2 = stack(inverse(pivot(block(2, 2) - dot3(m20, v02) - dot3(m21, v12), 2)))
-    for n, value in enumerate((i0, i1, i2, m10, m20, m21)):
-        out[n] = value
-    for n, value in enumerate((v01, v02, v12)):
-        out[6 + n, :SN] = value[0]
-        out[6 + n, SN:] = value[1]
+    done[0] = i0
+    done[1] = m10
+    done[2] = m20
+    put_pair(done.at[3], v01)
+    put_pair(done.at[4], v02)
+    rest[0] = block(1, 1) - dot3(m10, v01)
+    rest[1] = block(1, 2) - dot3(m10, v02)
+    rest[2] = block(2, 1) - dot3(m20, v01)
+    rest[3] = block(2, 2) - dot3(m20, v02)
+
+
+def factor_second(info, rest, done, last):
+    i1 = stack(inverse(with_ones(info, rest[0], 1)))
+    v12 = split(dot3(i1, split(rest[1])))
+    m21 = stack(rest[2])
+    done[0] = i1
+    done[1] = m21
+    put_pair(done.at[2], v12)
+    last[...] = rest[3] - dot3(m21, v12)
+
+
+def factor_third(info, last, done):
+    done[...] = stack(inverse(with_ones(info, last[...], 2)))
 
 
 def order_of(info, offset, axis, shape):
@@ -107,7 +132,10 @@
     return order
 
 
-def left_of(info, strips, got, left, panel):
+def left_of(info, strips, first, second, left, panel):
+    def pair(block):
+        return block[:SN], block[SN:]
+
     z = info[2]
     for k in range(COLS):
         place = lax.rem(z + k, COLS) * 64
@@ -120,38 +148,34 @@
     order = order_of(info, info[3] * 512, 0, (512, 1))
     c = [jnp.where(keep < info[4 + s], panel[:, SN * s:SN * s + SN], 0.0) for s in range(NSN)]
     l0 = stack(c[0])
-    l1 = stack(c[1] - dot3(l0, got(6)))
-    l2 = stack(c[2] - dot3(l0, got(7)) - dot3(l1, got(8)))
+    l1 = stack(c[1] - dot3(l0, pair(first[3])))
+    l2 = stack(c[2] - dot3(l0, pair(first[4])) - dot3(l1, pair(second[2])))
     live = jnp.concatenate([order, order], axis=0)
     for s, value in enumerate((l0, l1, l2)):
         left[:, SN * s:SN * s + SN] = jnp.where(live > s, value, jnp.zeros_like(value))
 
 
-def update_kernel(info, front, *refs, second):
-    own, other, blocks = refs[:4], refs[4:8], refs[8]
+def update_kernel(info, front, kept, *refs, again):
+    own, other, (first, second, third) = refs[:4], refs[4:8], refs[8:11]
     step = pl.program_id(0)
-
-    def got(n):
-        return blocks[n, :SN], blocks[n, SN:]
-
-    if second:
-        left, _, out, quarter, band = refs[9:]
+    if again:
+        left, _, out, quarter, band = refs[11:]
     else:
-        strips, (out, quarter, left, band, panel) = refs[9:18], refs[18:]
+        strips, (out, quarter, left, band, panel) = refs[11:20], refs[20:]
 
         @pl.when(step == 0)
         def _():
-            left_of(info, strips, got, left, panel)
-
-    half = info[8] if second else info[7]
+            left_of(info, strips, first, second, left, panel)
+
+    half = info[8] if again else info[7]
     width = band.shape[1]
     columns = pl.ds(pl.multiple_of(half * 512 + step * width, width), width)
     place_rows(band, own, other, info, columns)
     keep = lax.broadcasted_iota(jnp.int32, (SN, width), 0)
     r = [jnp.where(keep < info[4 + s], band[SN * s:SN * s + SN, :], 0.0) for s in range(NSN)]
-    s0 = split(dot3(blocks[0], split(r[0])))
-    s1 = split(dot3(blocks[1], split(r[1] - dot3(blocks[3], s0))))
-    s2 = split(dot3(blocks[2], split(r[2] - dot3(blocks[4], s0) - dot3(blocks[5], s1))))
+    s0 = split(dot3(first[0], split(r[0])))
+    s1 = split(dot3(second[0], split(r[1] - dot3(first[1], s0))))
+    s2 = split(dot3(third[...], split(r[2] - dot3(first[2], s0) - dot3(second[1], s1))))
     order = order_of(info, info[2] * 1024 + half * 512 + step * width, 1, (1, width))
     total = None
     for s, value in enumerate((s0, s1, s2)):
@@ -159,13 +183,12 @@
         masked = tuple(jnp.where(live, part, jnp.zeros_like(part)) for part in value)
         term = dot3(left[:, SN * s:SN * s + SN], masked)
         total = term if total is None else total + term
-    result = front[...] - total
-    out[...] = result
-    for i in range(2):
-        for j in range(width // 256):
-            quarter[128 * i:128 * i + 128, 128 * j:128 * j + 128] = result[
-                256 * i + 128:256 * i + 256, 256 * j + 128:256 * j + 256
-            ]
+    for i in range(4):
+        rows = slice(128 * i, 128 * i + 128)
+        result = front[rows, :] * kept[i:i + 1, columns] - total[rows]
+        out[rows, :] = result
+        if i % 2:
+            quarter[64 * (i - 1):64 * (i + 1), :] = result[:, 128:]
 
 
 VMEM_WHOLE = pl.BlockSpec(memory_space=pltpu.VMEM)
@@ -207,51 +230,66 @@
     return after[:4] + [far_high, far_low] + before[3:0:-1]
 
 
-def exchange(matrix, info, row_index, col_index):
+def exchange(front, kept, info, row_index, col_index):
     odd = (row_index // 2) % 2 == 1
     odd_col = col_index % 2 == 1
-    moved = lax.ppermute(matrix[384:512], "row", [(0, 1)])
-    panel = matrix[:, :PIV]
-    parts = [lax.ppermute(panel[64 * z:64 * z + 128], "col", [(0, z)]) for z in (2, 4, 6)]
-    strip = jnp.where(col_index == 0, panel[:128], parts[0] + parts[1] + parts[2])
-    strip = jnp.where(odd_col, lax.ppermute(strip[64:], "col", Z_ODD), strip[:64])
-
+    moved = lax.ppermute(front[384:512] * kept[3:4], "row", [(0, 1)])
     pieces = pl.pallas_call(
         pieces_kernel,
         grid_spec=pltpu.PrefetchScalarGridSpec(
             num_scalar_prefetch=1,
             grid=(),
-            in_specs=[VMEM_WHOLE] * 2,
-            out_specs=[VMEM_WHOLE] * CHIPS,
+            in_specs=[VMEM_WHOLE] * 3,
+            out_specs=[VMEM_WHOLE] * (2 * CHIPS),
         ),
-        out_shape=[jax.ShapeDtypeStruct((48, 1024), jnp.float32)] * CHIPS,
+        out_shape=[jax.ShapeDtypeStruct((48, width), jnp.float32) for width in [1024] * CHIPS + [PIV] * CHIPS],
         name="pieces",
-    )(info, matrix, moved)
-    parts = [lax.ppermute(pieces[q], "row", [(0, 2 * q), (1, 2 * q + 1)]) for q in range(1, CHIPS)]
-    piece = jnp.where(row_index < 2, pieces[0], sum(parts[1:], parts[0]))
-
-    core_piece = piece[:, :PIV]
-    parts = [lax.ppermute(core_piece, "col", [(0, z)]) for z in (4, 2, 6)]
+    )(info, front, kept, moved)
+
+    def from_first(parts):
+        return jnp.where(row_index < 2, parts[0], sum(parts[2:], parts[1]))
+
+    pairs = lambda q: [(0, 2 * q * COLS), (COLS, (2 * q + 1) * COLS)]
+    parts = [lax.ppermute(pieces[CHIPS + q], ("row", "col"), pairs(q)) for q in range(1, CHIPS)]
+    core_piece = from_first([pieces[CHIPS]] + parts)
+    parts = [lax.ppermute(core_piece, "col", [(0, z)]) for z in (2, 4, 6)]
     pivot_piece = jnp.where(col_index == 0, core_piece, parts[0] + parts[1] + parts[2])
     pivot_piece = jnp.where(odd_col, lax.ppermute(pivot_piece, "col", Z_ODD), pivot_piece)
 
+    strips = [front[128 * n:128 * n + 128, :PIV] * kept[n:n + 1, :PIV] for n in range(4)]
+    parts = [lax.ppermute(strips[n], "col", [(0, 2 * n)]) for n in range(1, 4)]
+    strip = jnp.where(col_index == 0, strips[0], parts[0] + parts[1] + parts[2])
+    strip = jnp.where(odd_col, lax.ppermute(strip[64:], "col", Z_ODD), strip[:64])
+
+    parts = [lax.ppermute(pieces[q], "row", [(0, 2 * q), (1, 2 * q + 1)]) for q in range(1, CHIPS)]
+    piece = from_first([pieces[0]] + parts)
+
     return gather_plane(piece, odd), gather_plane(pivot_piece, odd), gather_line(strip)
 
 
-def compute(info, matrix, band, pivot, strips):
-    blocks = pl.pallas_call(
-        factor_kernel,
+def factor(kernel, inputs, outputs, scratch=()):
+    return pl.pallas_call(
+        kernel,
         grid_spec=pltpu.PrefetchScalarGridSpec(
             num_scalar_prefetch=1,
             grid=(),
-            in_specs=[VMEM_WHOLE] * 8,
-            out_specs=VMEM_WHOLE,
-            scratch_shapes=[pltpu.VMEM((PIV, PIV), jnp.float32)],
+            in_specs=[VMEM_WHOLE] * (len(inputs) - 1),
+            out_specs=[VMEM_WHOLE] * len(outputs),
+            scratch_shapes=scratch,
         ),
-        out_shape=jax.ShapeDtypeStruct((9, 2 * SN, SN), jnp.bfloat16),
+        out_shape=outputs,
         name="factor",
-    )(info, *pivot[0], *pivot[1])
-
+    )(*inputs)
+
+
+def compute(info, front, kept, band, pivot, strips):
+    stacked = lambda *n: jax.ShapeDtypeStruct((*n, 2 * SN, SN), jnp.bfloat16)
+    square = lambda *n: jax.ShapeDtypeStruct((*n, SN, SN), jnp.float32)
+    first, rest = factor(
+        factor_first, (info, *pivot[0], *pivot[1]), [stacked(5), square(4)], [pltpu.VMEM((PIV, PIV), jnp.float32)]
+    )
+    second, last = factor(factor_second, (info, rest), [stacked(3), square()])
+    (third,) = factor(factor_third, (info, last), [stacked()])
     width = 256
 
     def update(which, *inputs):
@@ -261,11 +299,11 @@
         left_shape = (1024, PIV)
         specs = [VMEM_WHOLE, pl.BlockSpec(memory_space=pl.ANY)] if which else [VMEM_WHOLE] * len(inputs)
         return pl.pallas_call(
-            lambda *refs: update_kernel(*refs, second=which == 1),
+            lambda *refs: update_kernel(*refs, again=which == 1),
             grid_spec=pltpu.PrefetchScalarGridSpec(
                 num_scalar_prefetch=1,
                 grid=(2,),
-                in_specs=[pl.BlockSpec((512, width), at)] + [VMEM_WHOLE] * 9 + specs,
+                in_specs=[pl.BlockSpec((512, width), at)] + [VMEM_WHOLE] * 12 + specs,
                 out_specs=[
                     pl.BlockSpec((512, width), at),
                     pl.BlockSpec((256, width // 2), lambda j, info: (0, j)),
@@ -276,9 +314,9 @@
                 jax.ShapeDtypeStruct((512, 1024), jnp.float32),
                 jax.ShapeDtypeStruct((256, 256), jnp.float32),
             ] + [jax.ShapeDtypeStruct(left_shape, jnp.bfloat16)] * (1 - which),
-            input_output_aliases={12: 0} if which else {},
+            input_output_aliases={15: 0} if which else {},
             name="update",
-        )(info, matrix, *band[0], *band[1], blocks, *inputs)
+        )(info, front, kept, *band[0], *band[1], first, second, third, *inputs)
 
     partial, leaving, left = update(0, *strips)
     arriving = lax.ppermute(leaving, "depth", [(0, 1), (1, 0)])
@@ -293,15 +331,15 @@
     block_rows = row_index * 4 + jnp.arange(4)
     block_cols = col_index * 8 + jnp.arange(8)
     kept = ((block_mask[0] != 0) | (block_rows[:, None] == block_cols[None, :])).astype(jnp.float32)
-    kept = jnp.broadcast_to(kept[:, :, None], (4, 8, BLK)).reshape(4, 1, 1024)
-    matrix = (front_matrix[0].reshape(4, BLK, 1024) * kept).reshape(512, 1024)
+    kept = jnp.broadcast_to(kept[:, :, None], (4, 8, BLK)).reshape(4, 1024)
+    front = front_matrix[0]
     info = jnp.concatenate([
         jnp.stack([row_index // 4, row_index % 2, col_index, row_index]).astype(jnp.int32),
         supernode_width[0],
         jnp.stack([1 - depth_index, depth_index]).astype(jnp.int32),
     ])
-    panels = exchange(matrix, info, row_index, col_index)
-    return compute(info, matrix, *panels)
+    panels = exchange(front, kept, info, row_index, col_index)
+    return compute(info, front, kept, *panels)
 
 
 def solution(mesh):

time: 149 us -> 155 us (1.040)
  starting transfers between devices: 72.9 us -> 84.5 us
  waiting for transfers between devices: 23.7 us -> 17.3 us
  Pallas kernels: 34.4 us -> 39.9 us
  other arithmetic: 9.79 us -> 6.51 us
  local copies, waits for them, and re-layouts: 6.36 us -> 4.34 us
    ppermute x7 -> x14, starting transfers between devices: 22.4 us -> 34.7 us  [the longest x7 17.3 us: exchange(): lax.ppermute(pieces[CHIPS + q], ('row', 'col'), pairs(q))]
    pallas_call x3 -> x5, Pallas kernels: 30.9 us -> 36.1 us  [the longest x2 19.6 us: update(): pl.pallas_call(lambda *refs: update_kernel(*refs, again=which == 1), grid...]
    ppermute x7 -> x14, waiting for transfers between devices: 4.57 us -> 0.04 us  [the longest x7 0.02 us: exchange(): lax.ppermute(pieces[CHIPS + q], ('row', 'col'), pairs(q))]
    ppermute x2, starting transfers between devices: 1.49 us -> 5.38 us  [gather_plane(): far_odd = lax.ppermute(after[height:], 'row', X_DOWN)]
    ppermute x1, starting transfers between devices: 1.3 us -> 4.71 us  [exchange(): lax.ppermute(pivot_piece, 'col', Z_ODD)]
    ppermute x1, waiting for transfers between devices: 0.01 us -> 3.39 us  [exchange(): lax.ppermute(pivot_piece, 'col', Z_ODD)]
    ppermute x2, starting transfers between devices: 3.06 us -> 0.19 us  [gather_plane(): mate = lax.ppermute(piece, 'row', MATE)]
    ppermute x1, waiting for transfers between devices: 2.87 us -> 0.01 us  [exchange(): lax.ppermute(strip[64:], 'col', Z_ODD)]
  transfers between devices with their start and end apart: 43 -> 50, of which waited for: 11 -> 6; matrix products, arithmetic and copies ran while one was open for 5% -> 3% of each run, Pallas kernels for 14% -> 19%
where the time goes in v2:
time: 155 us; the launch traced here: 154 us
  starting transfers between devices  84.5 us (55%)
  Pallas kernels  39.9 us (26%)
  waiting for transfers between devices  17.3 us (11%)
  other arithmetic  6.51 us (4%)
  local copies, waits for them, and re-layouts  4.34 us (3%)
  between operations  1.71 us (1%)
    pallas_call x2, Pallas kernels, update(): pl.pallas_call(lambda *refs: update_kernel(*refs, again=which == 1), grid...  19.6 us
    ppermute x7, starting transfers between devices, exchange(): lax.ppermute(pieces[CHIPS + q], ('row', 'col'), pairs(q))  17.3 us
    pallas_call x3, Pallas kernels, factor(): pl.pallas_call(kernel, grid_spec=pltpu.PrefetchScalarGridSpec(num_scalar_...  16.5 us
    ppermute x8, starting transfers between devices, gather_plane(): return (own, [lax.ppermute(part, 'row', CORE) for part in own])  13.6 us
    ppermute x3, starting transfers between devices, exchange(): parts = [lax.ppermute(strips[n], 'col', [(0, 2 * n)]) for n in range(1, 4)]  12.3 us
    ppermute x7, starting transfers between devices, exchange(): lax.ppermute(pieces[q], 'row', [(0, 2 * q), (1, 2 * q + 1)])  11.1 us
    ppermute x2, starting transfers between devices, gather_plane(): far_odd = lax.ppermute(after[height:], 'row', X_DOWN)  5.38 us
    ppermute x2, starting transfers between devices, gather_plane(): after = lax.ppermute(pair, 'row', X_DOWN)  5.22 us
  transfers between devices with their start and end apart: 50, of which 6 were waited for; matrix products, arithmetic and copies ran while one was open for 3% of the time, Pallas kernels for 19%

profile of v2, /device:TPU:1, one launch (start us, length us, event | category | flops | bytes accessed | tf_op | source)
XLA Modules:
  0.0 154.2 jit_solution(14743605504252032070)
XLA Ops:
  4.1 1.3 slice_multiply_fusion.1
  5.4 9.7 %collective-permute-start.38 = (f32[128,768]{1,0:T(8,128)S(1)}, f32[128,768]{1,0:T(8,128)S(1)}, u32[]{:S(2)}, u32[]{:S(2)}) collective-permute-start(f32[128,768]{1,0:T(8,128)S(1)} %get-tuple-element.58), channel_id=1, source_target_pairs={{0,8},{1,9},{16,24},{17,25},{32,40},{33,41},{48,56},{49,57},{64,72... | collective-permute-start | bytes 1179656 | tf_op jit(solution)/shard_map/ppermute | solution.py:260
  15.1 1.3 collective-permute-start.39
  16.4 1.3 collective-permute-start.37
  19.2 3.9 %pieces.1 = (f32[48,1024]{1,0:T(8,128)}, f32[48,1024]{1,0:T(8,128)}, f32[48,1024]{1,0:T(8,128)}, f32[48,1024]{1,0:T(8,128)}, f32[48,1024]{1,0:T(8,128)}, /*index...) custom-call(s32[9]{0:T(128)} %concatenate.15.info.refs_0_, ...), custom_call_target="tpu_custom_call" | custom-call | tf_op jit(solution)/shard_map/pieces/pallas_call | solution.py:237
  23.2 4.4 %collective-permute-start.17 = (f32[48,768]{1,0:T(8,128)}, f32[48,768]{1,0:T(8,128)S(1)}, u32[]{:S(2)}, u32[]{:S(2)}) collective-permute-start(f32[48,768]{1,0:T(8,128)} %get-tuple-element.36), channel_id=1, source_target_pairs={{0,32},{16,48},{1,33},{17,49}} | collective-permute-start | bytes 442376 | tf_op jit(solution)/shard_map/ppermute | solution.py:253
  28.9 1.4 collective-permute-start.19
  31.7 6.3 %collective-permute-start.21 = (f32[48,768]{1,0:T(8,128)}, f32[48,768]{1,0:T(8,128)S(1)}, u32[]{:S(2)}, u32[]{:S(2)}) collective-permute-start(f32[48,768]{1,0:T(8,128)} %get-tuple-element.40), channel_id=1, source_target_pairs={{0,160},{16,176},{1,161},{17,177}} | collective-permute-start | bytes 442376 | tf_op jit(solution)/shard_map/ppermute | solution.py:253
  52.6 1.9 %collective-permute-start.5 = (f32[48,1024]{1,0:T(8,128)S(1)}, f32[48,1024]{1,0:T(8,128)S(1)}, u32[]{:S(2)}, u32[]{:S(2)}) collective-permute-start(f32[48,1024]{1,0:T(8,128)S(1)} %copy-done.30), channel_id=1, source_target_pairs={{0,160},{16,176},{1,161},{17,177},{2,162},{18,178},{3,163},{19,179... | collective-permute-start | bytes 589832 | tf_op jit(solution)/shard_map/ppermute | solution.py:264
  55.9 2.8 %collective-permute-start.7 = (f32[48,1024]{1,0:T(8,128)S(1)}, f32[48,1024]{1,0:T(8,128)S(1)}, u32[]{:S(2)}, u32[]{:S(2)}) collective-permute-start(f32[48,1024]{1,0:T(8,128)S(1)} %copy-done.28), channel_id=1, source_target_pairs={{0,224},{16,240},{1,225},{17,241},{2,226},{18,242},{3,227},{19,243... | collective-permute-start | bytes 589832 | tf_op jit(solution)/shard_map/ppermute | solution.py:264
  58.8 4.7 %collective-permute-start.27 = (f32[48,768]{1,0:T(8,128)S(1)}, f32[48,768]{1,0:T(8,128)S(1)}, u32[]{:S(2)}, u32[]{:S(2)}) collective-permute-start(f32[48,768]{1,0:T(8,128)S(1)} %add_select_fusion.1), channel_id=1, source_target_pairs={{0,2},{4,6},{8,10},{12,14},{1,3},{5,7},{9,11},{13,15},{16,18},{20,... | collective-permute-start | bytes 442376 | tf_op jit(solution)/shard_map/ppermute | solution.py:257
  63.8 3.4 %collective-permute-done.27 = f32[48,768]{1,0:T(8,128)S(1)} collective-permute-done((f32[48,768]{1,0:T(8,128)S(1)}, f32[48,768]{1,0:T(8,128)S(1)}, u32[]{:S(2)}, u32[]{:S(2)}) %collective-permute-start.27) | collective-permute-done | bytes 147488 | tf_op jit(solution)/shard_map/ppermute | solution.py:257
  67.3 2.5 %collective-permute-done.8 = f32[48,1024]{1,0:T(8,128)S(1)} collective-permute-done((f32[48,1024]{1,0:T(8,128)S(1)}, f32[48,1024]{1,0:T(8,128)S(1)}, u32[]{:S(2)}, u32[]{:S(2)}) %collective-permute-start.8) | collective-permute-done | bytes 196640 | tf_op jit(solution)/shard_map/ppermute | solution.py:212
  70.1 1.4 collective-permute-start.45
  71.5 2.6 %collective-permute-start.9 = (f32[96,1024]{1,0:T(8,128)S(1)}, f32[96,1024]{1,0:T(8,128)S(1)}, u32[]{:S(2)}, u32[]{:S(2)}) collective-permute-start(f32[96,1024]{1,0:T(8,128)S(1)} %pad_maximum_fusion.refs_3_), channel_id=1, source_target_pairs={{0,192},{16,208},{32,224},{48,240},{64,0},{80,16},{96,32},{112,48}... | collective-permute-start | bytes 1179656 | tf_op jit(solution)/shard_map/ppermute | solution.py:215
  74.3 1.9 %collective-permute-done.45.refs_21_ = f32[64,768]{1,0:T(8,128)S(1)} collective-permute-done((f32[64,768]{1,0:T(8,128)S(1)}, f32[64,768]{1,0:T(8,128)S(1)}, u32[]{:S(2)}, u32[]{:S(2)}) %collective-permute-start.45) | collective-permute-done | bytes 196640 | tf_op jit(solution)/shard_map/ppermute | solution.py:226
  76.2 2.6 %collective-permute-start.29 = (f32[96,768]{1,0:T(8,128)S(1)}, f32[96,768]{1,0:T(8,128)S(1)}, u32[]{:S(2)}, u32[]{:S(2)}) collective-permute-start(f32[96,768]{1,0:T(8,128)S(1)} %pad_maximum_fusion.1.refs_0_), channel_id=1, source_target_pairs={{0,192},{16,208},{32,224},{48,240},{64,0},{80,16},{96,32},{112,48}... | collective-permute-start | bytes 884744 | tf_op jit(solution)/shard_map/ppermute | solution.py:215
  79.1 2.6 %collective-permute-start.42 = (f32[64,768]{1,0:T(8,128)S(1)}, f32[64,768]{1,0:T(8,128)S(1)}, u32[]{:S(2)}, u32[]{:S(2)}) collective-permute-start(f32[64,768]{1,0:T(8,128)S(1)} %collective-permute-done.41.refs_15_), channel_id=1, source_target_pairs={{0,14},{2,0},{4,2},{6,4},{8,6},{10,8},{12,10},{14,12},{1,15},{3,1}... | collective-permute-start | bytes 589832 | tf_op jit(solution)/shard_map/ppermute | solution.py:227
  81.7 3.2 %collective-permute-done.46.refs_20_ = f32[64,768]{1,0:T(8,128)S(1)} collective-permute-done((f32[64,768]{1,0:T(8,128)S(1)}, f32[64,768]{1,0:T(8,128)S(1)}, u32[]{:S(2)}, u32[]{:S(2)}) %collective-permute-start.46) | collective-permute-done | bytes 196640 | tf_op jit(solution)/shard_map/ppermute | solution.py:226
  85.0 2.8 %collective-permute-start.12 = (f32[48,1024]{1,0:T(8,128)S(1)}, f32[48,1024]{1,0:T(8,128)S(1)}, u32[]{:S(2)}, u32[]{:S(2)}) collective-permute-start(f32[48,1024]{1,0:T(8,128)S(1)} %slice.88), channel_id=1, source_target_pairs={{0,192},{16,208},{32,224},{48,240},{64,0},{80,16},{96,32},{112,48}... | collective-permute-start | bytes 589832 | tf_op jit(solution)/shard_map/ppermute | solution.py:217
  87.8 9.0 %collective-permute-start.33 = (f32[96,768]{1,0:T(8,128)S(1)}, f32[96,768]{1,0:T(8,128)}, u32[]{:S(2)}, u32[]{:S(2)}) collective-permute-start(f32[96,768]{1,0:T(8,128)S(1)} %pad_maximum_fusion.1.refs_0_), channel_id=1, source_target_pairs={{0,16},{16,0},{32,48},{48,32},{64,80},{80,64},{96,112},{112,96},{1... | collective-permute-start | bytes 884744 | tf_op jit(solution)/shard_map/ppermute | solution.py:219
  97.2 2.5 %collective-permute-start.32 = (f32[48,768]{1,0:T(8,128)S(1)}, f32[48,768]{1,0:T(8,128)S(1)}, u32[]{:S(2)}, u32[]{:S(2)}) collective-permute-start(f32[48,768]{1,0:T(8,128)S(1)} %slice.90), channel_id=1, source_target_pairs={{0,192},{16,208},{32,224},{48,240},{64,0},{80,16},{96,32},{112,48}... | collective-permute-start | bytes 442376 | tf_op jit(solution)/shard_map/ppermute | solution.py:217
  101.3 2.2 %collective-permute-done.31 = f32[48,768]{1,0:T(8,128)S(1)} collective-permute-done((f32[48,768]{1,0:T(8,128)S(1)}, f32[48,768]{1,0:T(8,128)S(1)}, u32[]{:S(2)}, u32[]{:S(2)}) %collective-permute-start.31) | collective-permute-done | bytes 147488 | tf_op jit(solution)/shard_map/ppermute | solution.py:216
  103.5 1.5 collective-permute-start.47
  105.1 4.0 %collective-permute-done.43.refs_17_ = f32[64,768]{1,0:T(8,128)S(1)} collective-permute-done((f32[64,768]{1,0:T(8,128)S(1)}, f32[64,768]{1,0:T(8,128)S(1)}, u32[]{:S(2)}, u32[]{:S(2)}) %collective-permute-start.43) | collective-permute-done | bytes 196640 | tf_op jit(solution)/shard_map/ppermute | solution.py:227
  109.1 1.7 %collective-permute-start.13 = (f32[96,1024]{1,0:T(8,128)S(1)}, f32[96,1024]{1,0:T(8,128)S(1)}, u32[]{:S(2)}, u32[]{:S(2)}) collective-permute-start(f32[96,1024]{1,0:T(8,128)S(1)} %pad_maximum_fusion.refs_3_), channel_id=1, source_target_pairs={{0,16},{16,0},{32,48},{48,32},{64,80},{80,64},{96,112},{112,96},{1... | collective-permute-start | bytes 1179656 | tf_op jit(solution)/shard_map/ppermute | solution.py:219
  114.8 6.6 %factor.3 = (bf16[5,512,256]{2,1,0:T(8,128)(2,1)}, f32[4,256,256]{2,1,0:T(8,128)}) custom-call(s32[9]{0:T(128)} %concatenate.15.info.refs_0_, f32[96,768]{1,0:T(8,128)} %copy-done.8, f32[96,768]{1,0:T(8,128)} %copy-done.11, f32[96,768]{1,0:T(8,128)} %copy-done.12, f32[96,768]{1,0:T(8,128)} %copy-done.10, f32[96,768]{1,0:T(8,128)} %collective-permute-done.33.refs_4_, ...), custom_call_target="tpu_custom_call" | custom-call | tf_op jit(solution)/shard_map/factor/pallas_call | solution.py:271
  121.4 5.3 %factor.4 = (bf16[3,512,256]{2,1,0:T(8,128)(2,1)}, f32[256,256]{1,0:T(8,128)}) custom-call(s32[9]{0:T(128)} %concatenate.15.info.refs_0_, f32[4,256,256]{2,1,0:T(8,128)} %get-tuple-element.44.rest), custom_call_target="tpu_custom_call" | custom-call | tf_op jit(solution)/shard_map/factor/pallas_call | solution.py:271
  126.7 4.5 %factor.5.refs_13_ = bf16[512,256]{1,0:T(8,128)(2,1)} custom-call(s32[9]{0:T(128)} %concatenate.15.info.refs_0_, f32[256,256]{1,0:T(8,128)} %get-tuple-element.46.last), custom_call_target="tpu_custom_call" | custom-call | tf_op jit(solution)/shard_map/factor/pallas_call | solution.py:271
  132.4 10.3 %update.2 = (f32[512,1024]{1,0:T(8,128)}, f32[256,256]{1,0:T(8,128)}, bf16[1024,768]{1,0:T(8,128)(2,1)}) custom-call(s32[9]{0:T(128)} %concatenate.15.info.refs_0_, f32[512,1024]{1,0:T(8,128)} %bitcast.29, f32[4,1024]{1,0:T(4,128)} %bitcast.34, f32[96,1024]{1,0:T(8,128)} %copy-done, f32[96,1024]{1,0:T(8,128)} %copy-done.2, f32[96,1024]{1,0:T(8,128)} %copy-done.3, ...), custom_call_target="tpu_custom_call" | custom-call | tf_op jit(solution)/shard_map/update/pallas_call | solution.py:301
  143.2 9.3 %update.3 = (f32[512,1024]{1,0:T(8,128)}, f32[256,256]{1,0:T(8,128)}) custom-call(s32[9]{0:T(128)} %concatenate.15.info.refs_0_, f32[512,1024]{1,0:T(8,128)} %bitcast.30, f32[4,1024]{1,0:T(4,128)} %bitcast.35, f32[96,1024]{1,0:T(8,128)} %copy-done, f32[96,1024]{1,0:T(8,128)} %copy-done.2, f32[96,1024]{1,0:T(8,128)} %copy-done.3, ...), custom_call_target="tpu_custom_call", output_to_operand_aliasing={{0}: (15, {})} | custom-call | tf_op jit(solution)/shard_map/update/pallas_call | solution.py:301
  152.6 1.7 %add.106 = f32[256,256]{1,0:T(8,128)} add(f32[256,256]{1,0:T(8,128)} %get-tuple-element.50, f32[256,256]{1,0:T(8,128)S(1)} %collective-permute-done.49) | non-fusion elementwise | flops 65536 | bytes 786432 | tf_op jit(solution)/shard_map/add | solution.py:324
  (178 shorter events, 31.8 us)
Async XLA Ops:
  2.6 15.9 %collective-permute-start = (f32[128,1024]{1,0:T(8,128)S(1)}, f32[128,1024]{1,0:T(8,128)S(1)}, u32[]{:S(2)}, u32[]{:S(2)}) collective-permute-start(f32[128,1024]{1,0:T(8,128)S(1)} %bitcast_multiply_fusion), channel_id=1, source_target_pairs={{0,16},{1,17},{2,18},{3,19},{4,20},{5,21},{6,22},{7,23},{8,24},{9,... | collective-permute-start | bytes 1572872 | tf_op jit(solution)/shard_map/ppermute | solution.py:236
  5.4 23.5 %collective-permute-start.38 = (f32[128,768]{1,0:T(8,128)S(1)}, f32[128,768]{1,0:T(8,128)S(1)}, u32[]{:S(2)}, u32[]{:S(2)}) collective-permute-start(f32[128,768]{1,0:T(8,128)S(1)} %get-tuple-element.58), channel_id=1, source_target_pairs={{0,8},{1,9},{16,24},{17,25},{32,40},{33,41},{48,56},{49,57},{64,72... | collective-permute-start | bytes 1179656 | tf_op jit(solution)/shard_map/ppermute | solution.py:260
  15.1 15.3 %collective-permute-start.39 = (f32[128,768]{1,0:T(8,128)S(1)}, f32[128,768]{1,0:T(8,128)S(1)}, u32[]{:S(2)}, u32[]{:S(2)}) collective-permute-start(f32[128,768]{1,0:T(8,128)S(1)} %get-tuple-element.59), channel_id=1, source_target_pairs={{0,12},{1,13},{16,28},{17,29},{32,44},{33,45},{48,60},{49,61},{64,... | collective-permute-start | bytes 1179656 | tf_op jit(solution)/shard_map/ppermute | solution.py:260
  16.4 15.2 %collective-permute-start.37 = (f32[128,768]{1,0:T(8,128)S(1)}, f32[128,768]{1,0:T(8,128)S(1)}, u32[]{:S(2)}, u32[]{:S(2)}) collective-permute-start(f32[128,768]{1,0:T(8,128)S(1)} %get-tuple-element.60), channel_id=1, source_target_pairs={{0,4},{1,5},{16,20},{17,21},{32,36},{33,37},{48,52},{49,53},{64,68... | collective-permute-start | bytes 1179656 | tf_op jit(solution)/shard_map/ppermute | solution.py:260
  23.2 14.8 %collective-permute-start.17 = (f32[48,768]{1,0:T(8,128)}, f32[48,768]{1,0:T(8,128)S(1)}, u32[]{:S(2)}, u32[]{:S(2)}) collective-permute-start(f32[48,768]{1,0:T(8,128)} %get-tuple-element.36), channel_id=1, source_target_pairs={{0,32},{16,48},{1,33},{17,49}} | collective-permute-start | bytes 442376 | tf_op jit(solution)/shard_map/ppermute | solution.py:253
  27.5 11.8 %collective-permute-start.18 = (f32[48,768]{1,0:T(8,128)}, f32[48,768]{1,0:T(8,128)S(1)}, u32[]{:S(2)}, u32[]{:S(2)}) collective-permute-start(f32[48,768]{1,0:T(8,128)} %get-tuple-element.37), channel_id=1, source_target_pairs={{0,64},{16,80},{1,65},{17,81}} | collective-permute-start | bytes 442376 | tf_op jit(solution)/shard_map/ppermute | solution.py:253
  28.9 13.0 %collective-permute-start.19 = (f32[48,768]{1,0:T(8,128)}, f32[48,768]{1,0:T(8,128)S(1)}, u32[]{:S(2)}, u32[]{:S(2)}) collective-permute-start(f32[48,768]{1,0:T(8,128)} %get-tuple-element.38), channel_id=1, source_target_pairs={{0,96},{16,112},{1,97},{17,113}} | collective-permute-start | bytes 442376 | tf_op jit(solution)/shard_map/ppermute | solution.py:253
  30.4 12.8 %collective-permute-start.20 = (f32[48,768]{1,0:T(8,128)}, f32[48,768]{1,0:T(8,128)S(1)}, u32[]{:S(2)}, u32[]{:S(2)}) collective-permute-start(f32[48,768]{1,0:T(8,128)} %get-tuple-element.39), channel_id=1, source_target_pairs={{0,128},{16,144},{1,129},{17,145}} | collective-permute-start | bytes 442376 | tf_op jit(solution)/shard_map/ppermute | solution.py:253
  31.7 12.9 %collective-permute-start.21 = (f32[48,768]{1,0:T(8,128)}, f32[48,768]{1,0:T(8,128)S(1)}, u32[]{:S(2)}, u32[]{:S(2)}) collective-permute-start(f32[48,768]{1,0:T(8,128)} %get-tuple-element.40), channel_id=1, source_target_pairs={{0,160},{16,176},{1,161},{17,177}} | collective-permute-start | bytes 442376 | tf_op jit(solution)/shard_map/ppermute | solution.py:253
  38.0 7.9 %collective-permute-start.22 = (f32[48,768]{1,0:T(8,128)}, f32[48,768]{1,0:T(8,128)S(1)}, u32[]{:S(2)}, u32[]{:S(2)}) collective-permute-start(f32[48,768]{1,0:T(8,128)} %get-tuple-element.41), channel_id=1, source_target_pairs={{0,192},{16,208},{1,193},{17,209}} | collective-permute-start | bytes 442376 | tf_op jit(solution)/shard_map/ppermute | solution.py:253
  50.0 8.7 %collective-permute-start.3 = (f32[48,1024]{1,0:T(8,128)S(1)}, f32[48,1024]{1,0:T(8,128)S(1)}, u32[]{:S(2)}, u32[]{:S(2)}) collective-permute-start(f32[48,1024]{1,0:T(8,128)S(1)} %copy-done.32), channel_id=1, source_target_pairs={{0,96},{16,112},{1,97},{17,113},{2,98},{18,114},{3,99},{19,115},{4... | collective-permute-start | bytes 589832 | tf_op jit(solution)/shard_map/ppermute | solution.py:264
  52.6 10.9 %collective-permute-start.5 = (f32[48,1024]{1,0:T(8,128)S(1)}, f32[48,1024]{1,0:T(8,128)S(1)}, u32[]{:S(2)}, u32[]{:S(2)}) collective-permute-start(f32[48,1024]{1,0:T(8,128)S(1)} %copy-done.30), channel_id=1, source_target_pairs={{0,160},{16,176},{1,161},{17,177},{2,162},{18,178},{3,163},{19,179... | collective-permute-start | bytes 589832 | tf_op jit(solution)/shard_map/ppermute | solution.py:264
  54.5 9.0 %collective-permute-start.6 = (f32[48,1024]{1,0:T(8,128)S(1)}, f32[48,1024]{1,0:T(8,128)S(1)}, u32[]{:S(2)}, u32[]{:S(2)}) collective-permute-start(f32[48,1024]{1,0:T(8,128)S(1)} %copy-done.29), channel_id=1, source_target_pairs={{0,192},{16,208},{1,193},{17,209},{2,194},{18,210},{3,195},{19,211... | collective-permute-start | bytes 589832 | tf_op jit(solution)/shard_map/ppermute | solution.py:264
  55.9 7.7 %collective-permute-start.7 = (f32[48,1024]{1,0:T(8,128)S(1)}, f32[48,1024]{1,0:T(8,128)S(1)}, u32[]{:S(2)}, u32[]{:S(2)}) collective-permute-start(f32[48,1024]{1,0:T(8,128)S(1)} %copy-done.28), channel_id=1, source_target_pairs={{0,224},{16,240},{1,225},{17,241},{2,226},{18,242},{3,227},{19,243... | collective-permute-start | bytes 589832 | tf_op jit(solution)/shard_map/ppermute | solution.py:264
  58.7 11.4 %collective-permute-start.44 = (f32[64,768]{1,0:T(8,128)S(1)}, f32[64,768]{1,0:T(8,128)S(1)}, u32[]{:S(2)}, u32[]{:S(2)}) collective-permute-start(f32[64,768]{1,0:T(8,128)S(1)} %slice_select_fusion.refs_14_), channel_id=1, source_target_pairs={{0,2},{2,4},{4,6},{6,8},{8,10},{10,12},{12,14},{14,0},{1,3},{3,5},... | collective-permute-start | bytes 589832 | tf_op jit(solution)/shard_map/ppermute | solution.py:226
  58.8 8.4 %collective-permute-start.27 = (f32[48,768]{1,0:T(8,128)S(1)}, f32[48,768]{1,0:T(8,128)S(1)}, u32[]{:S(2)}, u32[]{:S(2)}) collective-permute-start(f32[48,768]{1,0:T(8,128)S(1)} %add_select_fusion.1), channel_id=1, source_target_pairs={{0,2},{4,6},{8,10},{12,14},{1,3},{5,7},{9,11},{13,15},{16,18},{20,... | collective-permute-start | bytes 442376 | tf_op jit(solution)/shard_map/ppermute | solution.py:257
  69.9 8.9 %collective-permute-start.10 = (f32[96,1024]{1,0:T(8,128)S(1)}, f32[96,1024]{1,0:T(8,128)S(1)}, u32[]{:S(2)}, u32[]{:S(2)}) collective-permute-start(f32[96,1024]{1,0:T(8,128)S(1)} %pad_maximum_fusion.refs_3_), channel_id=1, source_target_pairs={{0,64},{16,80},{32,96},{48,112},{64,128},{80,144},{96,160},{112,17... | collective-permute-start | bytes 1179656 | tf_op jit(solution)/shard_map/ppermute | solution.py:214
  70.0 9.0 %collective-permute-start.41 = (f32[64,768]{1,0:T(8,128)S(1)}, f32[64,768]{1,0:T(8,128)S(1)}, u32[]{:S(2)}, u32[]{:S(2)}) collective-permute-start(f32[64,768]{1,0:T(8,128)S(1)} %slice_select_fusion.refs_14_), channel_id=1, source_target_pairs={{0,14},{2,0},{4,2},{6,4},{8,6},{10,8},{12,10},{14,12},{1,15},{3,1}... | collective-permute-start | bytes 589832 | tf_op jit(solution)/shard_map/ppermute | solution.py:227
  74.2 13.6 %collective-permute-start.30 = (f32[96,768]{1,0:T(8,128)S(1)}, f32[96,768]{1,0:T(8,128)S(1)}, u32[]{:S(2)}, u32[]{:S(2)}) collective-permute-start(f32[96,768]{1,0:T(8,128)S(1)} %pad_maximum_fusion.1.refs_0_), channel_id=1, source_target_pairs={{0,64},{16,80},{32,96},{48,112},{64,128},{80,144},{96,160},{112,17... | collective-permute-start | bytes 884744 | tf_op jit(solution)/shard_map/ppermute | solution.py:214
  76.2 20.6 %collective-permute-start.29 = (f32[96,768]{1,0:T(8,128)S(1)}, f32[96,768]{1,0:T(8,128)S(1)}, u32[]{:S(2)}, u32[]{:S(2)}) collective-permute-start(f32[96,768]{1,0:T(8,128)S(1)} %pad_maximum_fusion.1.refs_0_), channel_id=1, source_target_pairs={{0,192},{16,208},{32,224},{48,240},{64,0},{80,16},{96,32},{112,48}... | collective-permute-start | bytes 884744 | tf_op jit(solution)/shard_map/ppermute | solution.py:215
  79.0 18.2 %collective-permute-start.11 = (f32[48,1024]{1,0:T(8,128)S(1)}, f32[48,1024]{1,0:T(8,128)S(1)}, u32[]{:S(2)}, u32[]{:S(2)}) collective-permute-start(f32[48,1024]{1,0:T(8,128)S(1)} %slice.87), channel_id=1, source_target_pairs={{0,64},{16,80},{32,96},{48,112},{64,128},{80,144},{96,160},{112,17... | collective-permute-start | bytes 589832 | tf_op jit(solution)/shard_map/ppermute | solution.py:216
  79.1 20.6 %collective-permute-start.42 = (f32[64,768]{1,0:T(8,128)S(1)}, f32[64,768]{1,0:T(8,128)S(1)}, u32[]{:S(2)}, u32[]{:S(2)}) collective-permute-start(f32[64,768]{1,0:T(8,128)S(1)} %collective-permute-done.41.refs_15_), channel_id=1, source_target_pairs={{0,14},{2,0},{4,2},{6,4},{8,6},{10,8},{12,10},{14,12},{1,15},{3,1}... | collective-permute-start | bytes 589832 | tf_op jit(solution)/shard_map/ppermute | solution.py:227
  85.0 15.5 %collective-permute-start.12 = (f32[48,1024]{1,0:T(8,128)S(1)}, f32[48,1024]{1,0:T(8,128)S(1)}, u32[]{:S(2)}, u32[]{:S(2)}) collective-permute-start(f32[48,1024]{1,0:T(8,128)S(1)} %slice.88), channel_id=1, source_target_pairs={{0,192},{16,208},{32,224},{48,240},{64,0},{80,16},{96,32},{112,48}... | collective-permute-start | bytes 589832 | tf_op jit(solution)/shard_map/ppermute | solution.py:217
  87.8 23.1 %collective-permute-start.33 = (f32[96,768]{1,0:T(8,128)S(1)}, f32[96,768]{1,0:T(8,128)}, u32[]{:S(2)}, u32[]{:S(2)}) collective-permute-start(f32[96,768]{1,0:T(8,128)S(1)} %pad_maximum_fusion.1.refs_0_), channel_id=1, source_target_pairs={{0,16},{16,0},{32,48},{48,32},{64,80},{80,64},{96,112},{112,96},{1... | collective-permute-start | bytes 884744 | tf_op jit(solution)/shard_map/ppermute | solution.py:219
  99.7 11.7 %collective-permute-start.36 = (f32[96,768]{1,0:T(8,128)S(1)}, f32[96,768]{1,0:T(8,128)S(1)}, u32[]{:S(2)}, u32[]{:S(2)}) collective-permute-start(f32[96,768]{1,0:T(8,128)S(1)} %collective-permute-done.30.refs_3_), channel_id=1, source_target_pairs={{0,16},{16,0},{32,48},{48,32},{64,80},{80,64},{96,112},{112,96},{1... | collective-permute-start | bytes 884744 | tf_op jit(solution)/shard_map/ppermute | solution.py:219
  100.4 11.2 %collective-permute-start.34 = (f32[96,768]{1,0:T(8,128)S(1)}, f32[96,768]{1,0:T(8,128)S(1)}, u32[]{:S(2)}, u32[]{:S(2)}) collective-permute-start(f32[96,768]{1,0:T(8,128)S(1)} %collective-permute-done.29.refs_1_), channel_id=1, source_target_pairs={{0,16},{16,0},{32,48},{48,32},{64,80},{80,64},{96,112},{112,96},{1... | collective-permute-start | bytes 884744 | tf_op jit(solution)/shard_map/ppermute | solution.py:219
  109.1 22.1 %collective-permute-start.13 = (f32[96,1024]{1,0:T(8,128)S(1)}, f32[96,1024]{1,0:T(8,128)S(1)}, u32[]{:S(2)}, u32[]{:S(2)}) collective-permute-start(f32[96,1024]{1,0:T(8,128)S(1)} %pad_maximum_fusion.refs_3_), channel_id=1, source_target_pairs={{0,16},{16,0},{32,48},{48,32},{64,80},{80,64},{96,112},{112,96},{1... | collective-permute-start | bytes 1179656 | tf_op jit(solution)/shard_map/ppermute | solution.py:219
  111.0 20.3 %collective-permute-start.16 = (f32[96,1024]{1,0:T(8,128)S(1)}, f32[96,1024]{1,0:T(8,128)S(1)}, u32[]{:S(2)}, u32[]{:S(2)}) collective-permute-start(f32[96,1024]{1,0:T(8,128)S(1)} %collective-permute-done.10.refs_6_), channel_id=1, source_target_pairs={{0,16},{16,0},{32,48},{48,32},{64,80},{80,64},{96,112},{112,96},{1... | collective-permute-start | bytes 1179656 | tf_op jit(solution)/shard_map/ppermute | solution.py:219
  111.5 19.8 %collective-permute-start.14 = (f32[96,1024]{1,0:T(8,128)S(1)}, f32[96,1024]{1,0:T(8,128)S(1)}, u32[]{:S(2)}, u32[]{:S(2)}) collective-permute-start(f32[96,1024]{1,0:T(8,128)S(1)} %collective-permute-done.9.refs_4_), channel_id=1, source_target_pairs={{0,16},{16,0},{32,48},{48,32},{64,80},{80,64},{96,112},{112,96},{1... | collective-permute-start | bytes 1179656 | tf_op jit(solution)/shard_map/ppermute | solution.py:219
  111.6 19.6 %collective-permute-start.15 = (f32[96,1024]{1,0:T(8,128)S(1)}, f32[96,1024]{1,0:T(8,128)S(1)}, u32[]{:S(2)}, u32[]{:S(2)}) collective-permute-start(f32[96,1024]{1,0:T(8,128)S(1)} %constant_dynamic-update-slice_fusion.refs_5_), channel_id=1, source_target_pairs={{0,16},{16,0},{32,48},{48,32},{64,80},{80,64},{96,112},{112,96},{1... | collective-permute-start | bytes 1179656 | tf_op jit(solution)/shard_map/ppermute | solution.py:219
  113.5 17.7 %collective-permute-start.48 = (f32[32,768]{1,0:T(8,128)}, f32[32,768]{1,0:T(8,128)}, u32[]{:S(2)}, u32[]{:S(2)}) collective-permute-start(f32[32,768]{1,0:T(8,128)} %slice.102), channel_id=1, source_target_pairs={{0,14},{2,0},{4,2},{6,4},{8,6},{10,8},{12,10},{14,12},{1,15},{3,1}... | collective-permute-start | bytes 294920 | tf_op jit(solution)/shard_map/ppermute | solution.py:229
  142.7 9.9 %collective-permute-start.49 = (f32[256,256]{1,0:T(8,128)}, f32[256,256]{1,0:T(8,128)S(1)}, u32[]{:S(2)}, u32[]{:S(2)}) collective-permute-start(f32[256,256]{1,0:T(8,128)} %get-tuple-element.51), channel_id=1, source_target_pairs={{0,1},{1,0},{2,3},{3,2},{4,5},{5,4},{6,7},{7,6},{8,9},{9,8},{10,11... | collective-permute-start | bytes 786440 | tf_op jit(solution)/shard_map/ppermute | solution.py:322
  (53 other events, 641.3 us)

commit v3 on v2

--- a/solution.py
+++ b/solution.py
@@ -64,13 +64,9 @@
 def pieces_kernel(info, front, kept, moved, *out):
     first = info[1] == 0
     for q in range(CHIPS):
-        high = front[32 * q:32 * q + 32, :] * kept[q // 4:q // 4 + 1, :]
+        out[q][:32, :] = front[32 * q:32 * q + 32, :] * kept[q // 4:q // 4 + 1, :]
         mine = front[256 + 16 * q:272 + 16 * q, :] * kept[2:3, :]
-        low = jnp.where(first, mine, moved[16 * q:16 * q + 16, :])
-        for target in (out[q], out[CHIPS + q]):
-            width = target.shape[1]
-            target[:32, :] = high[:, :width]
-            target[32:, :] = low[:, :width]
+        out[q][32:, :] = jnp.where(first, mine, moved[16 * q:16 * q + 16, :])
 
 
 def with_ones(info, value, i):
@@ -124,6 +120,13 @@
     done[...] = stack(inverse(with_ones(info, last[...], 2)))
 
 
+def factor_kernel(info, *refs):
+    first, second, third, rest, last, matrix = refs[8:]
+    factor_first(info, *refs[:8], first, rest, matrix)
+    factor_second(info, rest, second, last)
+    factor_third(info, last, third)
+
+
 def order_of(info, offset, axis, shape):
     ids = offset + lax.broadcasted_iota(jnp.int32, shape, axis)
     order = jnp.full(shape, NSN, jnp.int32)
@@ -132,18 +135,10 @@
     return order
 
 
-def left_of(info, strips, first, second, left, panel):
+def left_of(info, panel, first, second, left):
     def pair(block):
         return block[:SN], block[SN:]
 
-    z = info[2]
-    for k in range(COLS):
-        place = lax.rem(z + k, COLS) * 64
-        if k == 4:
-            panel[pl.ds(pl.multiple_of(place, 64), 32), :] = strips[4][...]
-            panel[pl.ds(pl.multiple_of(place + 32, 32), 32), :] = strips[5][...]
-        else:
-            panel[pl.ds(pl.multiple_of(place, 64), 64), :] = strips[k if k < 4 else k + 1][...]
     keep = lax.broadcasted_iota(jnp.int32, (512, SN), 1)
     order = order_of(info, info[3] * 512, 0, (512, 1))
     c = [jnp.where(keep < info[4 + s], panel[:, SN * s:SN * s + SN], 0.0) for s in range(NSN)]
@@ -161,11 +156,11 @@
     if again:
         left, _, out, quarter, band = refs[11:]
     else:
-        strips, (out, quarter, left, band, panel) = refs[11:20], refs[20:]
+        panel, out, quarter, left, band = refs[11:]
 
         @pl.when(step == 0)
         def _():
-            left_of(info, strips, first, second, left, panel)
+            left_of(info, panel, first, second, left)
 
     half = info[8] if again else info[7]
     width = band.shape[1]
@@ -202,8 +197,6 @@
 X_DOWN = each(ROWS, lambda i: (i - 4) % ROWS)
 MATE = each(ROWS, lambda i: i ^ 2)
 CORE = each(ROWS, lambda i: i ^ 1)
-Z_UP = each(COLS, lambda i: (i + 1) % COLS)
-Z_DOWN = each(COLS, lambda i: (i - 1) % COLS)
 Z_ODD = [(z, z + 1) for z in range(0, COLS, 2)]
 
 
@@ -219,17 +212,6 @@
     return own, [lax.ppermute(part, "row", CORE) for part in own]
 
 
-def gather_line(piece):
-    half = piece.shape[0] // 2
-    before, after = [piece], [piece]
-    for _ in range(1, 4):
-        before.append(lax.ppermute(before[-1], "col", Z_UP))
-        after.append(lax.ppermute(after[-1], "col", Z_DOWN))
-    far_high = lax.ppermute(before[3][:half], "col", Z_UP)
-    far_low = lax.ppermute(after[3][half:], "col", Z_DOWN)
-    return after[:4] + [far_high, far_low] + before[3:0:-1]
-
-
 def exchange(front, kept, info, row_index, col_index):
     odd = (row_index // 2) % 2 == 1
     odd_col = col_index % 2 == 1
@@ -240,56 +222,45 @@
             num_scalar_prefetch=1,
             grid=(),
             in_specs=[VMEM_WHOLE] * 3,
-            out_specs=[VMEM_WHOLE] * (2 * CHIPS),
+            out_specs=[VMEM_WHOLE] * CHIPS,
         ),
-        out_shape=[jax.ShapeDtypeStruct((48, width), jnp.float32) for width in [1024] * CHIPS + [PIV] * CHIPS],
+        out_shape=[jax.ShapeDtypeStruct((48, 1024), jnp.float32)] * CHIPS,
         name="pieces",
     )(info, front, kept, moved)
-
-    def from_first(parts):
-        return jnp.where(row_index < 2, parts[0], sum(parts[2:], parts[1]))
-
-    pairs = lambda q: [(0, 2 * q * COLS), (COLS, (2 * q + 1) * COLS)]
-    parts = [lax.ppermute(pieces[CHIPS + q], ("row", "col"), pairs(q)) for q in range(1, CHIPS)]
-    core_piece = from_first([pieces[CHIPS]] + parts)
+    parts = [lax.ppermute(pieces[q], "row", [(0, 2 * q), (1, 2 * q + 1)]) for q in range(1, CHIPS)]
+    piece = jnp.where(row_index < 2, pieces[0], sum(parts[1:], parts[0]))
+
+    core_piece = piece[:, :PIV]
     parts = [lax.ppermute(core_piece, "col", [(0, z)]) for z in (2, 4, 6)]
     pivot_piece = jnp.where(col_index == 0, core_piece, parts[0] + parts[1] + parts[2])
     pivot_piece = jnp.where(odd_col, lax.ppermute(pivot_piece, "col", Z_ODD), pivot_piece)
 
-    strips = [front[128 * n:128 * n + 128, :PIV] * kept[n:n + 1, :PIV] for n in range(4)]
-    parts = [lax.ppermute(strips[n], "col", [(0, 2 * n)]) for n in range(1, 4)]
-    strip = jnp.where(col_index == 0, strips[0], parts[0] + parts[1] + parts[2])
-    strip = jnp.where(odd_col, lax.ppermute(strip[64:], "col", Z_ODD), strip[:64])
-
-    parts = [lax.ppermute(pieces[q], "row", [(0, 2 * q), (1, 2 * q + 1)]) for q in range(1, CHIPS)]
-    piece = from_first([pieces[0]] + parts)
-
-    return gather_plane(piece, odd), gather_plane(pivot_piece, odd), gather_line(strip)
-
-
-def factor(kernel, inputs, outputs, scratch=()):
-    return pl.pallas_call(
-        kernel,
+    strips = [front[64 * z:64 * z + 64, :PIV] * kept[z // 2:z // 2 + 1, :PIV] for z in range(COLS)]
+    parts = [lax.ppermute(strips[z], "col", [(0, z)]) for z in range(1, COLS)]
+    strip = jnp.where(col_index == 0, strips[0], sum(parts[1:], parts[0]))
+    panel = lax.all_to_all(jnp.broadcast_to(strip[None], (COLS, 64, PIV)), "col", 0, 0).reshape(512, PIV)
+
+    return gather_plane(piece, odd), gather_plane(pivot_piece, odd), panel
+
+
+def compute(info, front, kept, band, pivot, panel):
+    stacked = lambda *n: jax.ShapeDtypeStruct((*n, 2 * SN, SN), jnp.bfloat16)
+    first, second, third = pl.pallas_call(
+        factor_kernel,
         grid_spec=pltpu.PrefetchScalarGridSpec(
             num_scalar_prefetch=1,
             grid=(),
-            in_specs=[VMEM_WHOLE] * (len(inputs) - 1),
-            out_specs=[VMEM_WHOLE] * len(outputs),
-            scratch_shapes=scratch,
+            in_specs=[VMEM_WHOLE] * 8,
+            out_specs=[VMEM_WHOLE] * 3,
+            scratch_shapes=[
+                pltpu.VMEM((4, SN, SN), jnp.float32),
+                pltpu.VMEM((SN, SN), jnp.float32),
+                pltpu.VMEM((PIV, PIV), jnp.float32),
+            ],
         ),
-        out_shape=outputs,
+        out_shape=[stacked(5), stacked(3), stacked()],
         name="factor",
-    )(*inputs)
-
-
-def compute(info, front, kept, band, pivot, strips):
-    stacked = lambda *n: jax.ShapeDtypeStruct((*n, 2 * SN, SN), jnp.bfloat16)
-    square = lambda *n: jax.ShapeDtypeStruct((*n, SN, SN), jnp.float32)
-    first, rest = factor(
-        factor_first, (info, *pivot[0], *pivot[1]), [stacked(5), square(4)], [pltpu.VMEM((PIV, PIV), jnp.float32)]
-    )
-    second, last = factor(factor_second, (info, rest), [stacked(3), square()])
-    (third,) = factor(factor_third, (info, last), [stacked()])
+    )(info, *pivot[0], *pivot[1])
     width = 256
 
     def update(which, *inputs):
@@ -308,7 +279,7 @@
                     pl.BlockSpec((512, width), at),
                     pl.BlockSpec((256, width // 2), lambda j, info: (0, j)),
                 ] + [VMEM_WHOLE] * (1 - which),
-                scratch_shapes=[pltpu.VMEM((PIV, width), jnp.float32)] + [pltpu.VMEM((512, PIV), jnp.float32)] * (1 - which),
+                scratch_shapes=[pltpu.VMEM((PIV, width), jnp.float32)],
             ),
             out_shape=[
                 jax.ShapeDtypeStruct((512, 1024), jnp.float32),
@@ -318,7 +289,7 @@
             name="update",
         )(info, front, kept, *band[0], *band[1], first, second, third, *inputs)
 
-    partial, leaving, left = update(0, *strips)
+    partial, leaving, left = update(0, panel)
     arriving = lax.ppermute(leaving, "depth", [(0, 1), (1, 0)])
     result, staying = update(1, left, partial)
     return result[None], staying + arriving

time: 155 us -> 159 us (1.026)
  waiting for transfers between devices: 17.3 us -> 40.5 us
  starting transfers between devices: 84.5 us -> 71.2 us
  Pallas kernels: 39.9 us -> 33.9 us
    ppermute x3, waiting for transfers between devices: 0.01 us -> 27.6 us  [exchange(): parts = [lax.ppermute(core_piece, 'col', [(0, z)]) for z in (2, 4, 6)]]
    ppermute x19 -> x7, starting transfers between devices: 38 us -> 14.8 us  [exchange(): parts = [lax.ppermute(strips[z], 'col', [(0, z)]) for z in range(1, COLS)]]
    ppermute x19 -> x7, waiting for transfers between devices: 9.14 us -> 0.02 us  [exchange(): parts = [lax.ppermute(strips[z], 'col', [(0, z)]) for z in range(1, COLS)]]
    pallas_call x3 -> x1, Pallas kernels: 16.5 us -> 10.7 us  [compute(): pl.pallas_call(factor_kernel, grid_spec=pltpu.PrefetchScalarGridSpec(num_...]
    ppermute x3, starting transfers between devices: 3.9 us -> 9.24 us  [exchange(): parts = [lax.ppermute(core_piece, 'col', [(0, z)]) for z in (2, 4, 6)]]
    ppermute x7, starting transfers between devices: 11.1 us -> 15.6 us  [exchange(): lax.ppermute(pieces[q], 'row', [(0, 2 * q), (1, 2 * q + 1)])]
    all_to_all x0 -> x1, starting transfers between devices: none -> 3.9 us  [exchange(): lax.all_to_all(jnp.broadcast_to(strip[None], (COLS, 64, PIV)), 'col', 0, 0)]
    ppermute x1, starting transfers between devices: 4.71 us -> 1.3 us  [exchange(): lax.ppermute(pivot_piece, 'col', Z_ODD)]
  transfers between devices with their start and end apart: 50 -> 39, of which waited for: 6 -> 9; matrix products, arithmetic and copies ran while one was open for 3% -> 3% of each run, Pallas kernels for 19% -> 15%
where the time goes in v3:
time: 159 us; the launch traced here: 158 us
  starting transfers between devices  71.2 us (45%)
  waiting for transfers between devices  40.5 us (25%)
  Pallas kernels  33.9 us (21%)
  other arithmetic  6.4 us (4%)
  local copies, waits for them, and re-layouts  4.56 us (3%)
    ppermute x3, waiting for transfers between devices, exchange(): parts = [lax.ppermute(core_piece, 'col', [(0, z)]) for z in (2, 4, 6)]  27.6 us
    pallas_call x2, Pallas kernels, update(): pl.pallas_call(lambda *refs: update_kernel(*refs, again=which == 1), grid...  19.6 us
    ppermute x7, starting transfers between devices, exchange(): lax.ppermute(pieces[q], 'row', [(0, 2 * q), (1, 2 * q + 1)])  15.6 us
    ppermute x7, starting transfers between devices, exchange(): parts = [lax.ppermute(strips[z], 'col', [(0, z)]) for z in range(1, COLS)]  14.8 us
    ppermute x8, starting transfers between devices, gather_plane(): return (own, [lax.ppermute(part, 'row', CORE) for part in own])  13.2 us
    pallas_call x1, Pallas kernels, compute(): pl.pallas_call(factor_kernel, grid_spec=pltpu.PrefetchScalarGridSpec(num_...  10.7 us
    ppermute x3, starting transfers between devices, exchange(): parts = [lax.ppermute(core_piece, 'col', [(0, z)]) for z in (2, 4, 6)]  9.24 us
    ppermute x2, starting transfers between devices, gather_plane(): far_odd = lax.ppermute(after[height:], 'row', X_DOWN)  5.44 us
  transfers between devices with their start and end apart: 39, of which 9 were waited for; matrix products, arithmetic and copies ran while one was open for 3% of the time, Pallas kernels for 15%

profile of v3, /device:TPU:1, one launch (start us, length us, event | category | flops | bytes accessed | tf_op | source)
XLA Modules:
  0.0 157.9 jit_solution(4592531241492307011)
XLA Ops:
  4.1 1.5 slice_multiply_fusion.5
  5.6 5.7 %collective-permute-start.31 = (f32[64,768]{1,0:T(8,128)S(1)}, f32[64,768]{1,0:T(8,128)S(1)}, u32[]{:S(2)}, u32[]{:S(2)}) collective-permute-start(f32[64,768]{1,0:T(8,128)S(1)} %get-tuple-element.40), channel_id=1, source_target_pairs={{0,4},{1,5},{16,20},{17,21},{32,36},{33,37},{48,52},{49,53},{64,68... | collective-permute-start | bytes 589832 | tf_op jit(solution)/shard_map/ppermute | solution.py:239
  11.4 2.0 %collective-permute-start.32 = (f32[64,768]{1,0:T(8,128)S(1)}, f32[64,768]{1,0:T(8,128)S(1)}, u32[]{:S(2)}, u32[]{:S(2)}) collective-permute-start(f32[64,768]{1,0:T(8,128)S(1)} %get-tuple-element.41), channel_id=1, source_target_pairs={{0,6},{1,7},{16,22},{17,23},{32,38},{33,39},{48,54},{49,55},{64,70... | collective-permute-start | bytes 589832 | tf_op jit(solution)/shard_map/ppermute | solution.py:239
  13.4 1.9 %collective-permute-start.36 = (f32[64,768]{1,0:T(8,128)S(1)}, f32[64,768]{1,0:T(8,128)S(1)}, u32[]{:S(2)}, u32[]{:S(2)}) collective-permute-start(f32[64,768]{1,0:T(8,128)S(1)} %get-tuple-element.46), channel_id=1, source_target_pairs={{0,14},{1,15},{16,30},{17,31},{32,46},{33,47},{48,62},{49,63},{64,... | collective-permute-start | bytes 589832 | tf_op jit(solution)/shard_map/ppermute | solution.py:239
  15.3 1.3 collective-permute-start.35
  18.7 3.5 %pieces.1 = (f32[48,1024]{1,0:T(8,128)}, f32[48,1024]{1,0:T(8,128)}, f32[48,1024]{1,0:T(8,128)}, f32[48,1024]{1,0:T(8,128)}, f32[48,1024]{1,0:T(8,128)}, /*index...) custom-call(s32[9]{0:T(128)} %concatenate.15.info.refs_0_, f32[512,1024]{1,0:T(8,128)} %bitcast.28, ...), custom_call_target="tpu_custom_call" | custom-call | tf_op jit(solution)/shard_map/pieces/pallas_call | solution.py:219
  23.5 1.3 collective-permute-start.30
  24.8 4.2 %collective-permute-start.1 = (f32[48,1024]{1,0:T(8,128)}, f32[48,1024]{1,0:T(8,128)S(1)}, u32[]{:S(2)}, u32[]{:S(2)}) collective-permute-start(f32[48,1024]{1,0:T(8,128)} %get-tuple-element.19), channel_id=1, source_target_pairs={{0,32},{16,48},{1,33},{17,49},{2,34},{18,50},{3,35},{19,51},{4,36}... | collective-permute-start | bytes 589832 | tf_op jit(solution)/shard_map/ppermute | solution.py:230
  29.1 1.3 collective-permute-start.2
  30.4 2.0 %collective-permute-start.3 = (f32[48,1024]{1,0:T(8,128)}, f32[48,1024]{1,0:T(8,128)S(1)}, u32[]{:S(2)}, u32[]{:S(2)}) collective-permute-start(f32[48,1024]{1,0:T(8,128)} %get-tuple-element.21), channel_id=1, source_target_pairs={{0,96},{16,112},{1,97},{17,113},{2,98},{18,114},{3,99},{19,115},{4... | collective-permute-start | bytes 589832 | tf_op jit(solution)/shard_map/ppermute | solution.py:230
  32.5 1.3 collective-permute-start.4
  33.8 4.2 %collective-permute-start.5 = (f32[48,1024]{1,0:T(8,128)}, f32[48,1024]{1,0:T(8,128)S(1)}, u32[]{:S(2)}, u32[]{:S(2)}) collective-permute-start(f32[48,1024]{1,0:T(8,128)} %get-tuple-element.23), channel_id=1, source_target_pairs={{0,160},{16,176},{1,161},{17,177},{2,162},{18,178},{3,163},{19,179... | collective-permute-start | bytes 589832 | tf_op jit(solution)/shard_map/ppermute | solution.py:230
  39.3 1.3 collective-permute-start.7
  42.9 3.9 %all-to-all-start = ((f32[8,64,768]{2,1,0:T(8,128)}), f32[8,64,768]{2,1,0:T(8,128)S(1)}, u32[]{:S(2)}, u32[]{:S(2)}) async-start(f32[8,64,768]{2,1,0:T(8,128)} %broadcast_in_dim.24), calls=%async_computation | async-start | bytes 3145728 | tf_op jit(solution)/shard_map/all_to_all | solution.py:241
  47.0 5.5 %collective-permute-start.19 = (f32[48,768]{1,0:T(8,128)S(1)}, f32[48,768]{1,0:T(8,128)S(1)}, u32[]{:S(2)}, u32[]{:S(2)}) collective-permute-start(f32[48,768]{1,0:T(8,128)S(1)} %slice.97), channel_id=1, source_target_pairs={{0,12},{1,13},{16,28},{17,29},{32,44},{33,45},{48,60},{49,61},{64,... | collective-permute-start | bytes 442376 | tf_op jit(solution)/shard_map/ppermute | solution.py:234
  52.4 2.5 %collective-permute-start.18 = (f32[48,768]{1,0:T(8,128)S(1)}, f32[48,768]{1,0:T(8,128)S(1)}, u32[]{:S(2)}, u32[]{:S(2)}) collective-permute-start(f32[48,768]{1,0:T(8,128)S(1)} %slice.97), channel_id=1, source_target_pairs={{0,8},{1,9},{16,24},{17,25},{32,40},{33,41},{48,56},{49,57},{64,72... | collective-permute-start | bytes 442376 | tf_op jit(solution)/shard_map/ppermute | solution.py:234
  56.2 14.2 %collective-permute-done.19 = f32[48,768]{1,0:T(8,128)S(1)} collective-permute-done((f32[48,768]{1,0:T(8,128)S(1)}, f32[48,768]{1,0:T(8,128)S(1)}, u32[]{:S(2)}, u32[]{:S(2)}) %collective-permute-start.19) | collective-permute-done | bytes 147488 | tf_op jit(solution)/shard_map/ppermute | solution.py:234
  70.4 9.4 %collective-permute-done.18 = f32[48,768]{1,0:T(8,128)S(1)} collective-permute-done((f32[48,768]{1,0:T(8,128)S(1)}, f32[48,768]{1,0:T(8,128)S(1)}, u32[]{:S(2)}, u32[]{:S(2)}) %collective-permute-start.18) | collective-permute-done | bytes 147488 | tf_op jit(solution)/shard_map/ppermute | solution.py:234
  79.8 4.0 %collective-permute-done.17 = f32[48,768]{1,0:T(8,128)S(1)} collective-permute-done((f32[48,768]{1,0:T(8,128)S(1)}, f32[48,768]{1,0:T(8,128)S(1)}, u32[]{:S(2)}, u32[]{:S(2)}) %collective-permute-start.17) | collective-permute-done | bytes 147488 | tf_op jit(solution)/shard_map/ppermute | solution.py:234
  85.3 3.9 %collective-permute-done.20 = f32[48,768]{1,0:T(8,128)S(1)} collective-permute-done((f32[48,768]{1,0:T(8,128)S(1)}, f32[48,768]{1,0:T(8,128)S(1)}, u32[]{:S(2)}, u32[]{:S(2)}) %collective-permute-start.20) | collective-permute-done | bytes 147488 | tf_op jit(solution)/shard_map/ppermute | solution.py:236
  89.4 1.9 %collective-permute-done.8 = f32[48,1024]{1,0:T(8,128)S(1)} collective-permute-done((f32[48,1024]{1,0:T(8,128)S(1)}, f32[48,1024]{1,0:T(8,128)S(1)}, u32[]{:S(2)}, u32[]{:S(2)}) %collective-permute-start.8) | collective-permute-done | bytes 196640 | tf_op jit(solution)/shard_map/ppermute | solution.py:205
  91.5 2.7 %collective-permute-start.9 = (f32[96,1024]{1,0:T(8,128)S(1)}, f32[96,1024]{1,0:T(8,128)S(1)}, u32[]{:S(2)}, u32[]{:S(2)}) collective-permute-start(f32[96,1024]{1,0:T(8,128)S(1)} %pad_maximum_fusion.refs_3_), channel_id=1, source_target_pairs={{0,192},{16,208},{32,224},{48,240},{64,0},{80,16},{96,32},{112,48}... | collective-permute-start | bytes 1179656 | tf_op jit(solution)/shard_map/ppermute | solution.py:208
  95.0 2.7 %collective-permute-start.22 = (f32[96,768]{1,0:T(8,128)S(1)}, f32[96,768]{1,0:T(8,128)S(1)}, u32[]{:S(2)}, u32[]{:S(2)}) collective-permute-start(f32[96,768]{1,0:T(8,128)S(1)} %pad_maximum_fusion.1.refs_0_), channel_id=1, source_target_pairs={{0,192},{16,208},{32,224},{48,240},{64,0},{80,16},{96,32},{112,48}... | collective-permute-start | bytes 884744 | tf_op jit(solution)/shard_map/ppermute | solution.py:208
  97.7 1.9 %collective-permute-done.10.refs_6_ = f32[96,1024]{1,0:T(8,128)S(1)} collective-permute-done((f32[96,1024]{1,0:T(8,128)S(1)}, f32[96,1024]{1,0:T(8,128)S(1)}, u32[]{:S(2)}, u32[]{:S(2)}) %collective-permute-start.10) | collective-permute-done | bytes 393248 | tf_op jit(solution)/shard_map/ppermute | solution.py:207
  99.8 2.7 %collective-permute-start.12 = (f32[48,1024]{1,0:T(8,128)S(1)}, f32[48,1024]{1,0:T(8,128)S(1)}, u32[]{:S(2)}, u32[]{:S(2)}) collective-permute-start(f32[48,1024]{1,0:T(8,128)S(1)} %slice.96), channel_id=1, source_target_pairs={{0,192},{16,208},{32,224},{48,240},{64,0},{80,16},{96,32},{112,48}... | collective-permute-start | bytes 589832 | tf_op jit(solution)/shard_map/ppermute | solution.py:210
  102.5 10.4 %collective-permute-start.26 = (f32[96,768]{1,0:T(8,128)S(1)}, f32[96,768]{1,0:T(8,128)S(1)}, u32[]{:S(2)}, u32[]{:S(2)}) collective-permute-start(f32[96,768]{1,0:T(8,128)S(1)} %pad_maximum_fusion.1.refs_0_), channel_id=1, source_target_pairs={{0,16},{16,0},{32,48},{48,32},{64,80},{80,64},{96,112},{112,96},{1... | collective-permute-start | bytes 884744 | tf_op jit(solution)/shard_map/ppermute | solution.py:212
  113.1 2.7 %collective-permute-start.25 = (f32[48,768]{1,0:T(8,128)S(1)}, f32[48,768]{1,0:T(8,128)S(1)}, u32[]{:S(2)}, u32[]{:S(2)}) collective-permute-start(f32[48,768]{1,0:T(8,128)S(1)} %slice.99), channel_id=1, source_target_pairs={{0,192},{16,208},{32,224},{48,240},{64,0},{80,16},{96,32},{112,48}... | collective-permute-start | bytes 442376 | tf_op jit(solution)/shard_map/ppermute | solution.py:210
  116.6 3.0 %collective-permute-done.24 = f32[48,768]{1,0:T(8,128)S(1)} collective-permute-done((f32[48,768]{1,0:T(8,128)S(1)}, f32[48,768]{1,0:T(8,128)S(1)}, u32[]{:S(2)}, u32[]{:S(2)}) %collective-permute-start.24) | collective-permute-done | bytes 147488 | tf_op jit(solution)/shard_map/ppermute | solution.py:209
  124.1 10.7 %factor.1 = (bf16[5,512,256]{2,1,0:T(8,128)(2,1)}, bf16[3,512,256]{2,1,0:T(8,128)(2,1)}, bf16[512,256]{1,0:T(8,128)(2,1)}) custom-call(s32[9]{0:T(128)} %concatenate.15.info.refs_0_, f32[96,768]{1,0:T(8,128)} %copy-done.6, f32[96,768]{1,0:T(8,128)} %copy-done.8, f32[96,768]{1,0:T(8,128)} %copy-done.9, f32[96,768]{1,0:T(8,128)} %copy-done.7, ...), custom_call_target="tpu_custom_call" | custom-call | tf_op jit(solution)/shard_map/factor/pallas_call | solution.py:248
  136.2 10.3 %update.2 = (f32[512,1024]{1,0:T(8,128)}, f32[256,256]{1,0:T(8,128)}, bf16[1024,768]{1,0:T(8,128)(2,1)}) custom-call(s32[9]{0:T(128)} %concatenate.15.info.refs_0_, f32[512,1024]{1,0:T(8,128)} %bitcast.30, f32[4,1024]{1,0:T(4,128)} %bitcast.36, f32[96,1024]{1,0:T(8,128)} %copy-done.1, f32[96,1024]{1,0:T(8,128)} %copy-done.3, f32[96,1024]{1,0:T(8,128)} %copy-done.4, ...), custom_call_target="tpu_custom_call" | custom-call | tf_op jit(solution)/shard_map/update/pallas_call | solution.py:272
  146.9 9.4 %update.3 = (f32[512,1024]{1,0:T(8,128)}, f32[256,256]{1,0:T(8,128)}) custom-call(s32[9]{0:T(128)} %concatenate.15.info.refs_0_, f32[512,1024]{1,0:T(8,128)} %bitcast.31, f32[4,1024]{1,0:T(4,128)} %bitcast.37, f32[96,1024]{1,0:T(8,128)} %copy-done.1, f32[96,1024]{1,0:T(8,128)} %copy-done.3, f32[96,1024]{1,0:T(8,128)} %copy-done.4, ...), custom_call_target="tpu_custom_call", output_to_operand_aliasing={{0}: (15, {})} | custom-call | tf_op jit(solution)/shard_map/update/pallas_call | solution.py:272
  156.2 1.7 %add.98 = f32[256,256]{1,0:T(8,128)} add(f32[256,256]{1,0:T(8,128)} %get-tuple-element.32, f32[256,256]{1,0:T(8,128)S(1)} %collective-permute-done.37) | non-fusion elementwise | flops 65536 | bytes 786432 | tf_op jit(solution)/shard_map/add | solution.py:295
  (115 shorter events, 21.4 us)
Async XLA Ops:
  2.6 14.7 %collective-permute-start = (f32[128,1024]{1,0:T(8,128)S(1)}, f32[128,1024]{1,0:T(8,128)S(1)}, u32[]{:S(2)}, u32[]{:S(2)}) collective-permute-start(f32[128,1024]{1,0:T(8,128)S(1)} %bitcast_multiply_fusion), channel_id=1, source_target_pairs={{0,16},{1,17},{2,18},{3,19},{4,20},{5,21},{6,22},{7,23},{8,24},{9,... | collective-permute-start | bytes 1572872 | tf_op jit(solution)/shard_map/ppermute | solution.py:218
  5.6 16.6 %collective-permute-start.31 = (f32[64,768]{1,0:T(8,128)S(1)}, f32[64,768]{1,0:T(8,128)S(1)}, u32[]{:S(2)}, u32[]{:S(2)}) collective-permute-start(f32[64,768]{1,0:T(8,128)S(1)} %get-tuple-element.40), channel_id=1, source_target_pairs={{0,4},{1,5},{16,20},{17,21},{32,36},{33,37},{48,52},{49,53},{64,68... | collective-permute-start | bytes 589832 | tf_op jit(solution)/shard_map/ppermute | solution.py:239
  11.4 12.1 %collective-permute-start.32 = (f32[64,768]{1,0:T(8,128)S(1)}, f32[64,768]{1,0:T(8,128)S(1)}, u32[]{:S(2)}, u32[]{:S(2)}) collective-permute-start(f32[64,768]{1,0:T(8,128)S(1)} %get-tuple-element.41), channel_id=1, source_target_pairs={{0,6},{1,7},{16,22},{17,23},{32,38},{33,39},{48,54},{49,55},{64,70... | collective-permute-start | bytes 589832 | tf_op jit(solution)/shard_map/ppermute | solution.py:239
  13.4 11.4 %collective-permute-start.36 = (f32[64,768]{1,0:T(8,128)S(1)}, f32[64,768]{1,0:T(8,128)S(1)}, u32[]{:S(2)}, u32[]{:S(2)}) collective-permute-start(f32[64,768]{1,0:T(8,128)S(1)} %get-tuple-element.46), channel_id=1, source_target_pairs={{0,14},{1,15},{16,30},{17,31},{32,46},{33,47},{48,62},{49,63},{64,... | collective-permute-start | bytes 589832 | tf_op jit(solution)/shard_map/ppermute | solution.py:239
  15.3 13.8 %collective-permute-start.35 = (f32[64,768]{1,0:T(8,128)S(1)}, f32[64,768]{1,0:T(8,128)S(1)}, u32[]{:S(2)}, u32[]{:S(2)}) collective-permute-start(f32[64,768]{1,0:T(8,128)S(1)} %get-tuple-element.47), channel_id=1, source_target_pairs={{0,12},{1,13},{16,28},{17,29},{32,44},{33,45},{48,60},{49,61},{64,... | collective-permute-start | bytes 589832 | tf_op jit(solution)/shard_map/ppermute | solution.py:239
  17.3 13.1 %collective-permute-start.34 = (f32[64,768]{1,0:T(8,128)S(1)}, f32[64,768]{1,0:T(8,128)S(1)}, u32[]{:S(2)}, u32[]{:S(2)}) collective-permute-start(f32[64,768]{1,0:T(8,128)S(1)} %get-tuple-element.48), channel_id=1, source_target_pairs={{0,10},{1,11},{16,26},{17,27},{32,42},{33,43},{48,58},{49,59},{64,... | collective-permute-start | bytes 589832 | tf_op jit(solution)/shard_map/ppermute | solution.py:239
  22.2 10.3 %collective-permute-start.33 = (f32[64,768]{1,0:T(8,128)S(1)}, f32[64,768]{1,0:T(8,128)S(1)}, u32[]{:S(2)}, u32[]{:S(2)}) collective-permute-start(f32[64,768]{1,0:T(8,128)S(1)} %get-tuple-element.49), channel_id=1, source_target_pairs={{0,8},{1,9},{16,24},{17,25},{32,40},{33,41},{48,56},{49,57},{64,72... | collective-permute-start | bytes 589832 | tf_op jit(solution)/shard_map/ppermute | solution.py:239
  23.5 10.3 %collective-permute-start.30 = (f32[64,768]{1,0:T(8,128)S(1)}, f32[64,768]{1,0:T(8,128)S(1)}, u32[]{:S(2)}, u32[]{:S(2)}) collective-permute-start(f32[64,768]{1,0:T(8,128)S(1)} %get-tuple-element.50), channel_id=1, source_target_pairs={{0,2},{1,3},{16,18},{17,19},{32,34},{33,35},{48,50},{49,51},{64,66... | collective-permute-start | bytes 589832 | tf_op jit(solution)/shard_map/ppermute | solution.py:239
  24.8 13.1 %collective-permute-start.1 = (f32[48,1024]{1,0:T(8,128)}, f32[48,1024]{1,0:T(8,128)S(1)}, u32[]{:S(2)}, u32[]{:S(2)}) collective-permute-start(f32[48,1024]{1,0:T(8,128)} %get-tuple-element.19), channel_id=1, source_target_pairs={{0,32},{16,48},{1,33},{17,49},{2,34},{18,50},{3,35},{19,51},{4,36}... | collective-permute-start | bytes 589832 | tf_op jit(solution)/shard_map/ppermute | solution.py:230
  29.1 10.2 %collective-permute-start.2 = (f32[48,1024]{1,0:T(8,128)}, f32[48,1024]{1,0:T(8,128)S(1)}, u32[]{:S(2)}, u32[]{:S(2)}) collective-permute-start(f32[48,1024]{1,0:T(8,128)} %get-tuple-element.20), channel_id=1, source_target_pairs={{0,64},{16,80},{1,65},{17,81},{2,66},{18,82},{3,67},{19,83},{4,68}... | collective-permute-start | bytes 589832 | tf_op jit(solution)/shard_map/ppermute | solution.py:230
  30.4 16.4 %collective-permute-start.3 = (f32[48,1024]{1,0:T(8,128)}, f32[48,1024]{1,0:T(8,128)S(1)}, u32[]{:S(2)}, u32[]{:S(2)}) collective-permute-start(f32[48,1024]{1,0:T(8,128)} %get-tuple-element.21), channel_id=1, source_target_pairs={{0,96},{16,112},{1,97},{17,113},{2,98},{18,114},{3,99},{19,115},{4... | collective-permute-start | bytes 589832 | tf_op jit(solution)/shard_map/ppermute | solution.py:230
  32.5 14.3 %collective-permute-start.4 = (f32[48,1024]{1,0:T(8,128)}, f32[48,1024]{1,0:T(8,128)S(1)}, u32[]{:S(2)}, u32[]{:S(2)}) collective-permute-start(f32[48,1024]{1,0:T(8,128)} %get-tuple-element.22), channel_id=1, source_target_pairs={{0,128},{16,144},{1,129},{17,145},{2,130},{18,146},{3,131},{19,147... | collective-permute-start | bytes 589832 | tf_op jit(solution)/shard_map/ppermute | solution.py:230
  33.8 13.0 %collective-permute-start.5 = (f32[48,1024]{1,0:T(8,128)}, f32[48,1024]{1,0:T(8,128)S(1)}, u32[]{:S(2)}, u32[]{:S(2)}) collective-permute-start(f32[48,1024]{1,0:T(8,128)} %get-tuple-element.23), channel_id=1, source_target_pairs={{0,160},{16,176},{1,161},{17,177},{2,162},{18,178},{3,163},{19,179... | collective-permute-start | bytes 589832 | tf_op jit(solution)/shard_map/ppermute | solution.py:230
  38.0 8.9 %collective-permute-start.6 = (f32[48,1024]{1,0:T(8,128)}, f32[48,1024]{1,0:T(8,128)S(1)}, u32[]{:S(2)}, u32[]{:S(2)}) collective-permute-start(f32[48,1024]{1,0:T(8,128)} %get-tuple-element.24), channel_id=1, source_target_pairs={{0,192},{16,208},{1,193},{17,209},{2,194},{18,210},{3,195},{19,211... | collective-permute-start | bytes 589832 | tf_op jit(solution)/shard_map/ppermute | solution.py:230
  39.3 7.5 %collective-permute-start.7 = (f32[48,1024]{1,0:T(8,128)}, f32[48,1024]{1,0:T(8,128)S(1)}, u32[]{:S(2)}, u32[]{:S(2)}) collective-permute-start(f32[48,1024]{1,0:T(8,128)} %get-tuple-element.25), channel_id=1, source_target_pairs={{0,224},{16,240},{1,225},{17,241},{2,226},{18,242},{3,227},{19,243... | collective-permute-start | bytes 589832 | tf_op jit(solution)/shard_map/ppermute | solution.py:230
  42.9 92.0 %all-to-all-start = ((f32[8,64,768]{2,1,0:T(8,128)}), f32[8,64,768]{2,1,0:T(8,128)S(1)}, u32[]{:S(2)}, u32[]{:S(2)}) async-start(f32[8,64,768]{2,1,0:T(8,128)} %broadcast_in_dim.24), calls=%async_computation | async-start | bytes 3145728 | tf_op jit(solution)/shard_map/all_to_all | solution.py:241
  47.0 23.5 %collective-permute-start.19 = (f32[48,768]{1,0:T(8,128)S(1)}, f32[48,768]{1,0:T(8,128)S(1)}, u32[]{:S(2)}, u32[]{:S(2)}) collective-permute-start(f32[48,768]{1,0:T(8,128)S(1)} %slice.97), channel_id=1, source_target_pairs={{0,12},{1,13},{16,28},{17,29},{32,44},{33,45},{48,60},{49,61},{64,... | collective-permute-start | bytes 442376 | tf_op jit(solution)/shard_map/ppermute | solution.py:234
  52.4 27.3 %collective-permute-start.18 = (f32[48,768]{1,0:T(8,128)S(1)}, f32[48,768]{1,0:T(8,128)S(1)}, u32[]{:S(2)}, u32[]{:S(2)}) collective-permute-start(f32[48,768]{1,0:T(8,128)S(1)} %slice.97), channel_id=1, source_target_pairs={{0,8},{1,9},{16,24},{17,25},{32,40},{33,41},{48,56},{49,57},{64,72... | collective-permute-start | bytes 442376 | tf_op jit(solution)/shard_map/ppermute | solution.py:234
  54.9 28.9 %collective-permute-start.17 = (f32[48,768]{1,0:T(8,128)S(1)}, f32[48,768]{1,0:T(8,128)S(1)}, u32[]{:S(2)}, u32[]{:S(2)}) collective-permute-start(f32[48,768]{1,0:T(8,128)S(1)} %slice.97), channel_id=1, source_target_pairs={{0,4},{1,5},{16,20},{17,21},{32,36},{33,37},{48,52},{49,53},{64,68... | collective-permute-start | bytes 442376 | tf_op jit(solution)/shard_map/ppermute | solution.py:234
  91.4 8.2 %collective-permute-start.10 = (f32[96,1024]{1,0:T(8,128)S(1)}, f32[96,1024]{1,0:T(8,128)S(1)}, u32[]{:S(2)}, u32[]{:S(2)}) collective-permute-start(f32[96,1024]{1,0:T(8,128)S(1)} %pad_maximum_fusion.refs_3_), channel_id=1, source_target_pairs={{0,64},{16,80},{32,96},{48,112},{64,128},{80,144},{96,160},{112,17... | collective-permute-start | bytes 1179656 | tf_op jit(solution)/shard_map/ppermute | solution.py:207
  91.5 8.2 %collective-permute-start.9 = (f32[96,1024]{1,0:T(8,128)S(1)}, f32[96,1024]{1,0:T(8,128)S(1)}, u32[]{:S(2)}, u32[]{:S(2)}) collective-permute-start(f32[96,1024]{1,0:T(8,128)S(1)} %pad_maximum_fusion.refs_3_), channel_id=1, source_target_pairs={{0,192},{16,208},{32,224},{48,240},{64,0},{80,16},{96,32},{112,48}... | collective-permute-start | bytes 1179656 | tf_op jit(solution)/shard_map/ppermute | solution.py:208
  94.9 18.0 %collective-permute-start.23 = (f32[96,768]{1,0:T(8,128)S(1)}, f32[96,768]{1,0:T(8,128)S(1)}, u32[]{:S(2)}, u32[]{:S(2)}) collective-permute-start(f32[96,768]{1,0:T(8,128)S(1)} %pad_maximum_fusion.1.refs_0_), channel_id=1, source_target_pairs={{0,64},{16,80},{32,96},{48,112},{64,128},{80,144},{96,160},{112,17... | collective-permute-start | bytes 884744 | tf_op jit(solution)/shard_map/ppermute | solution.py:207
  95.0 18.0 %collective-permute-start.22 = (f32[96,768]{1,0:T(8,128)S(1)}, f32[96,768]{1,0:T(8,128)S(1)}, u32[]{:S(2)}, u32[]{:S(2)}) collective-permute-start(f32[96,768]{1,0:T(8,128)S(1)} %pad_maximum_fusion.1.refs_0_), channel_id=1, source_target_pairs={{0,192},{16,208},{32,224},{48,240},{64,0},{80,16},{96,32},{112,48}... | collective-permute-start | bytes 884744 | tf_op jit(solution)/shard_map/ppermute | solution.py:208
  99.6 16.2 %collective-permute-start.11 = (f32[48,1024]{1,0:T(8,128)S(1)}, f32[48,1024]{1,0:T(8,128)S(1)}, u32[]{:S(2)}, u32[]{:S(2)}) collective-permute-start(f32[48,1024]{1,0:T(8,128)S(1)} %slice.95), channel_id=1, source_target_pairs={{0,64},{16,80},{32,96},{48,112},{64,128},{80,144},{96,160},{112,17... | collective-permute-start | bytes 589832 | tf_op jit(solution)/shard_map/ppermute | solution.py:209
  99.8 16.7 %collective-permute-start.12 = (f32[48,1024]{1,0:T(8,128)S(1)}, f32[48,1024]{1,0:T(8,128)S(1)}, u32[]{:S(2)}, u32[]{:S(2)}) collective-permute-start(f32[48,1024]{1,0:T(8,128)S(1)} %slice.96), channel_id=1, source_target_pairs={{0,192},{16,208},{32,224},{48,240},{64,0},{80,16},{96,32},{112,48}... | collective-permute-start | bytes 589832 | tf_op jit(solution)/shard_map/ppermute | solution.py:210
  102.5 18.0 %collective-permute-start.26 = (f32[96,768]{1,0:T(8,128)S(1)}, f32[96,768]{1,0:T(8,128)S(1)}, u32[]{:S(2)}, u32[]{:S(2)}) collective-permute-start(f32[96,768]{1,0:T(8,128)S(1)} %pad_maximum_fusion.1.refs_0_), channel_id=1, source_target_pairs={{0,16},{16,0},{32,48},{48,32},{64,80},{80,64},{96,112},{112,96},{1... | collective-permute-start | bytes 884744 | tf_op jit(solution)/shard_map/ppermute | solution.py:212
  113.1 7.6 %collective-permute-start.25 = (f32[48,768]{1,0:T(8,128)S(1)}, f32[48,768]{1,0:T(8,128)S(1)}, u32[]{:S(2)}, u32[]{:S(2)}) collective-permute-start(f32[48,768]{1,0:T(8,128)S(1)} %slice.99), channel_id=1, source_target_pairs={{0,192},{16,208},{32,224},{48,240},{64,0},{80,16},{96,32},{112,48}... | collective-permute-start | bytes 442376 | tf_op jit(solution)/shard_map/ppermute | solution.py:210
  119.6 15.2 %collective-permute-start.13 = (f32[96,1024]{1,0:T(8,128)S(1)}, f32[96,1024]{1,0:T(8,128)S(1)}, u32[]{:S(2)}, u32[]{:S(2)}) collective-permute-start(f32[96,1024]{1,0:T(8,128)S(1)} %pad_maximum_fusion.refs_3_), channel_id=1, source_target_pairs={{0,16},{16,0},{32,48},{48,32},{64,80},{80,64},{96,112},{112,96},{1... | collective-permute-start | bytes 1179656 | tf_op jit(solution)/shard_map/ppermute | solution.py:212
  120.5 14.3 %collective-permute-start.16 = (f32[96,1024]{1,0:T(8,128)S(1)}, f32[96,1024]{1,0:T(8,128)}, u32[]{:S(2)}, u32[]{:S(2)}) collective-permute-start(f32[96,1024]{1,0:T(8,128)S(1)} %collective-permute-done.10.refs_6_), channel_id=1, source_target_pairs={{0,16},{16,0},{32,48},{48,32},{64,80},{80,64},{96,112},{112,96},{1... | collective-permute-start | bytes 1179656 | tf_op jit(solution)/shard_map/ppermute | solution.py:212
  120.6 14.2 %collective-permute-start.14 = (f32[96,1024]{1,0:T(8,128)S(1)}, f32[96,1024]{1,0:T(8,128)}, u32[]{:S(2)}, u32[]{:S(2)}) collective-permute-start(f32[96,1024]{1,0:T(8,128)S(1)} %collective-permute-done.9.refs_4_), channel_id=1, source_target_pairs={{0,16},{16,0},{32,48},{48,32},{64,80},{80,64},{96,112},{112,96},{1... | collective-permute-start | bytes 1179656 | tf_op jit(solution)/shard_map/ppermute | solution.py:212
  121.1 13.7 %collective-permute-start.15 = (f32[96,1024]{1,0:T(8,128)S(1)}, f32[96,1024]{1,0:T(8,128)}, u32[]{:S(2)}, u32[]{:S(2)}) collective-permute-start(f32[96,1024]{1,0:T(8,128)S(1)} %constant_dynamic-update-slice_fusion.refs_5_), channel_id=1, source_target_pairs={{0,16},{16,0},{32,48},{48,32},{64,80},{80,64},{96,112},{112,96},{1... | collective-permute-start | bytes 1179656 | tf_op jit(solution)/shard_map/ppermute | solution.py:212
  146.4 9.8 %collective-permute-start.37 = (f32[256,256]{1,0:T(8,128)}, f32[256,256]{1,0:T(8,128)S(1)}, u32[]{:S(2)}, u32[]{:S(2)}) collective-permute-start(f32[256,256]{1,0:T(8,128)} %get-tuple-element.33), channel_id=1, source_target_pairs={{0,1},{1,0},{2,3},{3,2},{4,5},{5,4},{6,7},{7,6},{8,9},{9,8},{10,11... | collective-permute-start | bytes 786440 | tf_op jit(solution)/shard_map/ppermute | solution.py:293
  (24 other events, 254.8 us)
